TPU v7x, 256 devices: a whole 4x4x8 slice. The times are simulated.
256 devices in a mesh: dp: 8 (over x, core), section: 4 (over y), seq: 8 (over z).
Axes of the slice: x: 4, y: 4, z: 8, core: 2. Of those that a mesh axis runs over, the one named last changes fastest.
Arguments:
- clips_in: bfloat16 [16, 8, 128, 1280], P('dp', None, 'seq'), may hold values from -6 to 6
- w_qkv: bfloat16 [4, 1280, 1920], P('section'), may hold values from -1 to 1
- w_out: bfloat16 [4, 640, 1280], P('section'), may hold values from -0.25 to 0.25
- out_cotangent: bfloat16 [16, 8, 128, 1280], P('dp', 'seq'), may hold values from -0.046875 to 0.046875
Outputs:
- section_outputs: bfloat16 [4, 16, 8, 128, 1280], P('section', 'dp', 'seq')
- grad_qkv: float32 [4, 1280, 1920], P('section', ('dp', 'seq'))
- grad_out_t: float32 [4, 1280, 640], P('section', ('dp', 'seq'))
All inputs are finite; a program needn't handle non-finite values.
Results may differ from a plain program's by a relative error of at most 0.025.
Values may be sent and summed in bfloat16 or wider, within the bound.
A program may use at most 128 MiB of HBM per device.

v0:
```python
import math

import jax
import jax.numpy as jnp
from jax import lax
from jax.sharding import PartitionSpec as P

HEADS = 10


norm_eps = 1e-05


def shortened(x):

    def short(part):
        return part.astype(jnp.bfloat16) if part.dtype == jnp.float32 else part

    return jax.tree.map(short, x)


def shifted(x, axis, by):
    count = lax.axis_size(axis)
    pairs = [(i, i + by) for i in range(count) if 0 <= i + by < count]
    return lax.ppermute(x, axis, pairs)


def normalize(token_rows):
    values = token_rows.astype(jnp.float32)
    centred = values - jnp.mean(values, axis=-1, keepdims=True)
    inverse = lax.rsqrt(jnp.mean(centred * centred, axis=-1, keepdims=True) + norm_eps)
    return (centred * inverse, inverse)


def split_heads(packed, groups, heads):
    row_count, all_cols = packed.shape
    head_block = all_cols // 3
    length = row_count // groups
    head_dim = head_block // heads
    pieces = [
        packed[:, piece_idx * head_block : (piece_idx + 1) * head_block].reshape(
            groups, length, heads, head_dim
        )
        for piece_idx in range(3)
    ]
    return (pieces[0], pieces[1], pieces[2])


def softmax_rows(query_heads, key_heads, score_scale):
    scores = (
        jnp.einsum("glhe,gmhe->ghlm", query_heads, key_heads, preferred_element_type=jnp.float32)
        * score_scale
    )
    row_max = jnp.max(scores, axis=-1, keepdims=True)
    exp_scores = jnp.exp(scores - row_max)
    return exp_scores / jnp.sum(exp_scores, axis=-1, keepdims=True)


def project(token_rows, weight_qkv, groups, heads):
    unit_rows, _ = normalize(token_rows)
    normed = unit_rows.astype(jnp.bfloat16)
    packed = jnp.dot(normed, weight_qkv, preferred_element_type=jnp.float32).astype(jnp.bfloat16)
    query_heads, key_heads, value_heads = split_heads(packed, groups, heads)
    score_scale = 1.0 / math.sqrt(query_heads.shape[-1])
    probs_low = softmax_rows(query_heads, key_heads, score_scale).astype(jnp.bfloat16)
    mixed_heads = jnp.einsum(
        "ghlm,gmhe->glhe", probs_low, value_heads, preferred_element_type=jnp.float32
    )
    return (packed, mixed_heads.astype(jnp.bfloat16).reshape(token_rows.shape[0], -1))


def backward_rows(
    token_rows, packed, mixed_heads, weight_qkv, weight_out, grad_rows, groups, heads
):
    unit_rows, inverse = normalize(token_rows)
    normed = unit_rows.astype(jnp.bfloat16)
    d_mixed = jnp.einsum(
        "rc,ec->re", grad_rows, weight_out, preferred_element_type=jnp.float32
    ).astype(jnp.bfloat16)
    grad_out_term = jnp.einsum(
        "rc,re->ce", grad_rows, mixed_heads, preferred_element_type=jnp.float32
    )
    query_heads, key_heads, value_heads = split_heads(packed, groups, heads)
    score_scale = 1.0 / math.sqrt(query_heads.shape[-1])
    probs = softmax_rows(query_heads, key_heads, score_scale)
    probs_low = probs.astype(jnp.bfloat16)
    d_heads = d_mixed.reshape(query_heads.shape)
    d_values = jnp.einsum("ghlm,glhe->gmhe", probs_low, d_heads, preferred_element_type=jnp.float32)
    d_probs = jnp.einsum(
        "glhe,gmhe->ghlm", d_heads, value_heads, preferred_element_type=jnp.float32
    )
    d_scores = (probs * (d_probs - jnp.sum(probs * d_probs, axis=-1, keepdims=True))).astype(
        jnp.bfloat16
    )
    d_query = (
        jnp.einsum("ghlm,gmhe->glhe", d_scores, key_heads, preferred_element_type=jnp.float32)
        * score_scale
    )
    d_keys = (
        jnp.einsum("ghlm,glhe->gmhe", d_scores, query_heads, preferred_element_type=jnp.float32)
        * score_scale
    )
    row_count = token_rows.shape[0]
    d_packed = jnp.concatenate(
        [
            d_query.reshape(row_count, -1),
            d_keys.reshape(row_count, -1),
            d_values.reshape(row_count, -1),
        ],
        axis=-1,
    ).astype(jnp.bfloat16)
    grad_qkv_term = jnp.einsum("rd,rc->dc", normed, d_packed, preferred_element_type=jnp.float32)
    d_normed = jnp.einsum("rc,dc->rd", d_packed, weight_qkv, preferred_element_type=jnp.float32)
    d_inside = inverse * (
        d_normed
        - jnp.mean(d_normed, axis=-1, keepdims=True)
        - unit_rows * jnp.mean(d_normed * unit_rows, axis=-1, keepdims=True)
    )
    back_rows = (grad_rows.astype(jnp.float32) + d_inside).astype(jnp.bfloat16)
    return (back_rows, grad_qkv_term, grad_out_term)


def to_token_rows(section_block, parity):
    seq_count, frames_dev, patches_dev, model_width = section_block.shape
    if parity == 0:
        return (
            section_block.reshape(seq_count * frames_dev, patches_dev, model_width)
            .transpose(1, 0, 2)
            .reshape(-1, model_width)
        )
    return section_block.transpose(1, 0, 2, 3).reshape(-1, model_width)


def from_token_rows(token_rows, block_shape, parity):
    seq_count, frames_dev, patches_dev, model_width = block_shape
    if parity == 0:
        return (
            token_rows.reshape(patches_dev, seq_count * frames_dev, model_width)
            .transpose(1, 0, 2)
            .reshape(block_shape)
        )
    return token_rows.reshape(frames_dev, seq_count, patches_dev, model_width).transpose(1, 0, 2, 3)


def group_count(block_shape, parity):
    return block_shape[2] if parity == 0 else block_shape[1]


def place(buffer, new_value, active, micro_slot):
    current = lax.dynamic_index_in_dim(buffer, micro_slot, 0, keepdims=False)
    return lax.dynamic_update_index_in_dim(
        buffer, jnp.where(active, new_value, current), micro_slot, 0
    )


def local(clips_in, w_qkv, w_out, out_cotangent):
    seq_count = lax.axis_size("seq")
    section_count = lax.axis_size("section")
    section_id = lax.axis_index("section")
    section_kind = section_id % 2
    micro_count = clips_in.shape[0]
    frames_dev = out_cotangent.shape[1]
    patches_dev = clips_in.shape[2]
    model_width = clips_in.shape[3]
    weight_qkv = w_qkv[0]
    weight_out = w_out[0]
    inner_width = weight_out.shape[0]
    block_shape = (seq_count, frames_dev, patches_dev, model_width)
    token_count = seq_count * frames_dev * patches_dev
    inputs_blocks = clips_in.reshape((micro_count,) + block_shape)
    cotangent_blocks = out_cotangent.reshape(
        micro_count, frames_dev, seq_count, patches_dev, model_width
    ).transpose(0, 2, 1, 3, 4)
    tick_count = micro_count + section_count - 1

    def forward_spare(section_block):
        return (
            jnp.zeros(block_shape, jnp.bfloat16),
            jnp.zeros((token_count, 3 * inner_width), jnp.bfloat16),
            jnp.zeros((token_count, inner_width), jnp.bfloat16),
        )

    def forward_on(parity):

        def run_section(section_block):
            token_rows = to_token_rows(section_block, parity)
            packed, mixed_heads = project(
                token_rows, weight_qkv, group_count(block_shape, parity), HEADS
            )
            result = (
                token_rows.astype(jnp.float32)
                + jnp.dot(mixed_heads, weight_out, preferred_element_type=jnp.float32)
            ).astype(jnp.bfloat16)
            return (from_token_rows(result, block_shape, parity), packed, mixed_heads)

        return run_section

    forward_branches = [forward_spare, forward_on(0), forward_on(1)]

    def forward_tick(tick_index, loop_state):
        received, saved_inputs, saved_packed, saved_mixed, section_outs = loop_state
        micro_index = tick_index - section_id
        active = (micro_index >= 0) & (micro_index < micro_count)
        micro_slot = jnp.clip(micro_index, 0, micro_count - 1)
        fresh_input = lax.dynamic_index_in_dim(inputs_blocks, micro_slot, 0, keepdims=False)
        section_in = jnp.where(section_id == 0, fresh_input, received)
        branch = jnp.where(active, 1 + section_kind, 0)
        result, packed, mixed_heads = lax.switch(branch, forward_branches, section_in)
        relaid = jax.tree.map(
            lambda part, own: part.astype(own.dtype),
            lax.all_to_all(shortened(result), "seq", split_axis=0, concat_axis=0, tiled=True),
            result,
        )
        frame_split = jnp.where(section_kind == 0, relaid, result)
        saved_inputs = place(saved_inputs, section_in, active, micro_slot)
        section_outs = place(section_outs, frame_split, active, micro_slot)
        received = jax.tree.map(
            lambda part, own: part.astype(own.dtype),
            shifted(shortened(relaid), "section", 1),
            relaid,
        )
        return (received, saved_inputs, saved_packed, saved_mixed, section_outs)

    packed_shape = (1, 1, 1)
    mixed_shape = (1, 1, 1)
    start_state = (
        jnp.zeros(block_shape, jnp.bfloat16),
        jnp.zeros((micro_count,) + block_shape, jnp.bfloat16),
        jnp.zeros(packed_shape, jnp.bfloat16),
        jnp.zeros(mixed_shape, jnp.bfloat16),
        jnp.zeros((micro_count,) + block_shape, jnp.bfloat16),
    )
    _, saved_inputs, saved_packed, saved_mixed, section_outs = lax.fori_loop(
        0, tick_count, forward_tick, start_state
    )

    def backward_spare(section_block, grad_block, micro_slot):
        return (
            jnp.zeros(block_shape, jnp.bfloat16),
            jnp.zeros((model_width, 3 * inner_width), jnp.float32),
            jnp.zeros((model_width, inner_width), jnp.float32),
        )

    def backward_on(parity):

        def run_back(section_block, grad_block, micro_slot):
            token_rows = to_token_rows(section_block, parity)
            groups = group_count(block_shape, parity)
            packed, mixed_heads = project(token_rows, weight_qkv, groups, HEADS)
            back_rows, grad_qkv_term, grad_out_term = backward_rows(
                token_rows,
                packed,
                mixed_heads,
                weight_qkv,
                weight_out,
                to_token_rows(grad_block, parity),
                groups,
                HEADS,
            )
            return (from_token_rows(back_rows, block_shape, parity), grad_qkv_term, grad_out_term)

        return run_back

    backward_branches = [backward_spare, backward_on(0), backward_on(1)]

    def backward_tick(tick_index, loop_state):
        received, total_qkv, total_out = loop_state
        micro_index = tick_index - (section_count - 1 - section_id)
        active = (micro_index >= 0) & (micro_index < micro_count)
        micro_slot = jnp.clip(micro_index, 0, micro_count - 1)
        seed_grad = lax.dynamic_index_in_dim(cotangent_blocks, micro_slot, 0, keepdims=False)
        grad_in = jnp.where(section_id == section_count - 1, seed_grad, received)
        section_block = lax.dynamic_index_in_dim(saved_inputs, micro_slot, 0, keepdims=False)
        branch = jnp.where(active, 1 + section_kind, 0)
        back_block, grad_qkv_term, grad_out_term = lax.switch(
            branch, backward_branches, section_block, grad_in, micro_slot
        )
        total_qkv = total_qkv + grad_qkv_term
        total_out = total_out + grad_out_term
        relaid = jax.tree.map(
            lambda part, own: part.astype(own.dtype),
            lax.all_to_all(shortened(back_block), "seq", split_axis=0, concat_axis=0, tiled=True),
            back_block,
        )
        received = jax.tree.map(
            lambda part, own: part.astype(own.dtype),
            shifted(shortened(relaid), "section", -1),
            relaid,
        )
        return (received, total_qkv, total_out)

    back_start = (
        jnp.zeros(block_shape, jnp.bfloat16),
        jnp.zeros((model_width, 3 * inner_width), jnp.float32),
        jnp.zeros((model_width, inner_width), jnp.float32),
    )
    _, total_qkv, total_out = lax.fori_loop(0, tick_count, backward_tick, back_start)
    shard_qkv, shard_out = (
        lax.psum_scatter(total_qkv, ("dp", "seq"), scatter_dimension=0, tiled=True),
        lax.psum_scatter(total_out, ("dp", "seq"), scatter_dimension=0, tiled=True),
    )
    outputs_local = section_outs.transpose(0, 2, 1, 3, 4).reshape(
        micro_count, frames_dev, seq_count * patches_dev, model_width
    )
    return (outputs_local[None], shard_qkv[None], shard_out[None])


def solution(mesh):
    return jax.shard_map(
        local,
        mesh=mesh,
        in_specs=(
            P("dp", None, "seq", None),
            P("section", None, None),
            P("section", None, None),
            P("dp", "seq", None, None),
        ),
        out_specs=(
            P("section", "dp", "seq", None, None),
            P("section", ("dp", "seq"), None),
            P("section", ("dp", "seq"), None),
        ),
        check_vma=False,
    )
```

profile of v0, /device:TPU:2, one launch (start us, length us, event | category | flops | bytes accessed | tf_op | source)
XLA Modules:
  0.0 753.6 jit_solution(2892451297610640468)
XLA Ops:
  10.3 194.7 %while.39 = (s32[]{:T(128)}, bf16[8,1,16,1280]{3,2,1,0:T(8,128)(2,1)S(1)}, bf16[2,8,1,16,1280]{4,1,3,2,0:T(8,128)(2,1)S(1)}, bf16[2,8,1,16,1280]{4,3,1,2,0:T(8,1...) while((s32[]{:T(128)}, ...), condition=%wide.region_12.13_spmd, body=%wide.region_0.12_spmd.sunk | while | flops 906036864 | bytes 28853620 | solution.py:233
  11.5 18.8 %conditional.5 = (bf16[8,1,16,1280]{3,2,1,0:T(8,128)(2,1)}) conditional(s32[]{:T(128)} %clamp.21, () %tuple.146, (bf16[8,1,16,1280]{3,2,1,0:T(8,128)(2,1)S(1)}, bf16[1280,1920]{1,0:T(8,128)(2,1)}, bf16[640,1280]{1,0:T(8,128)(2,1)}) %tuple.147, (bf16[8,1,16,1280]{3,2,1,0:T(8,128)(2,1)S(1)}, bf16[1280,1920]{1,0:T(8,128)(2,1)}, ...), branch_computations={%region_1.1_spmd, %region_2.6_spmd, %region_7.11_spmd} | conditional | flops 905381504 | bytes 21643812 | solution.py:208
  30.3 8.5 %all-to-all-start = ((bf16[8,1,16,1280]{3,2,1,0:T(8,128)(2,1)}), bf16[8,1,16,1280]{3,2,1,0:T(8,128)(2,1)S(1)}, u32[]{:S(2)}, u32[]{:S(2)}) async-start(bf16[8,1,16,1280]{3,2,1,0:T(8,128)(2,1)} %get-tuple-element.957), calls=%async_computation | async-start | bytes 655360 | tf_op jit(solution)/shard_map/while/body/eval_jaxpr/all_to_all | solution.py:211
  39.9 12.2 %all-to-all-done = bf16[8,1,16,1280]{3,2,1,0:T(8,128)(2,1)S(1)} async-done(((bf16[8,1,16,1280]{3,2,1,0:T(8,128)(2,1)}), bf16[8,1,16,1280]{3,2,1,0:T(8,128)(2,1)S(1)}, u32[]{:S(2)}, u32[]{:S(2)}) %all-to-all-start) | async-done | bytes 327712 | tf_op jit(solution)/shard_map/while/body/eval_jaxpr/all_to_all | solution.py:211
  60.0 18.8 %conditional.5 = (bf16[8,1,16,1280]{3,2,1,0:T(8,128)(2,1)}) conditional(s32[]{:T(128)} %clamp.21, () %tuple.146, (bf16[8,1,16,1280]{3,2,1,0:T(8,128)(2,1)S(1)}, bf16[1280,1920]{1,0:T(8,128)(2,1)}, bf16[640,1280]{1,0:T(8,128)(2,1)}) %tuple.147, (bf16[8,1,16,1280]{3,2,1,0:T(8,128)(2,1)S(1)}, bf16[1280,1920]{1,0:T(8,128)(2,1)}, ...), branch_computations={%region_1.1_spmd, %region_2.6_spmd, %region_7.11_spmd} | conditional | flops 905381504 | bytes 21643812 | solution.py:208
  83.4 10.3 %all-to-all-done = bf16[8,1,16,1280]{3,2,1,0:T(8,128)(2,1)S(1)} async-done(((bf16[8,1,16,1280]{3,2,1,0:T(8,128)(2,1)}), bf16[8,1,16,1280]{3,2,1,0:T(8,128)(2,1)S(1)}, u32[]{:S(2)}, u32[]{:S(2)}) %all-to-all-start) | async-done | bytes 327712 | tf_op jit(solution)/shard_map/while/body/eval_jaxpr/all_to_all | solution.py:211
  105.9 10.0 %all-to-all-done = bf16[8,1,16,1280]{3,2,1,0:T(8,128)(2,1)S(1)} async-done(((bf16[8,1,16,1280]{3,2,1,0:T(8,128)(2,1)}), bf16[8,1,16,1280]{3,2,1,0:T(8,128)(2,1)S(1)}, u32[]{:S(2)}, u32[]{:S(2)}) %all-to-all-start) | async-done | bytes 327712 | tf_op jit(solution)/shard_map/while/body/eval_jaxpr/all_to_all | solution.py:211
  115.9 15.2 %collective-permute-start = (bf16[8,1,16,1280]{3,2,1,0:T(8,128)(2,1)S(1)}, bf16[8,1,16,1280]{3,2,1,0:T(8,128)(2,1)S(1)}, u32[]{:S(2)}, u32[]{:S(2)}) collective-permute-start(bf16[8,1,16,1280]{3,2,1,0:T(8,128)(2,1)S(1)} %all-to-all-done), channel_id=1, source_target_pairs={{0,8},{8,16},{16,24},{1,9},{9,17},{17,25},{2,10},{10,18},{18,26},{... | collective-permute-start | bytes 983048 | tf_op jit(solution)/shard_map/while/body/eval_jaxpr/ppermute | solution.py:25
  142.0 10.0 %all-to-all-done = bf16[8,1,16,1280]{3,2,1,0:T(8,128)(2,1)S(1)} async-done(((bf16[8,1,16,1280]{3,2,1,0:T(8,128)(2,1)}), bf16[8,1,16,1280]{3,2,1,0:T(8,128)(2,1)S(1)}, u32[]{:S(2)}, u32[]{:S(2)}) %all-to-all-start) | async-done | bytes 327712 | tf_op jit(solution)/shard_map/while/body/eval_jaxpr/all_to_all | solution.py:211
  168.0 10.0 %all-to-all-done = bf16[8,1,16,1280]{3,2,1,0:T(8,128)(2,1)S(1)} async-done(((bf16[8,1,16,1280]{3,2,1,0:T(8,128)(2,1)}), bf16[8,1,16,1280]{3,2,1,0:T(8,128)(2,1)S(1)}, u32[]{:S(2)}, u32[]{:S(2)}) %all-to-all-start) | async-done | bytes 327712 | tf_op jit(solution)/shard_map/while/body/eval_jaxpr/all_to_all | solution.py:211
  178.0 22.4 %collective-permute-start = (bf16[8,1,16,1280]{3,2,1,0:T(8,128)(2,1)S(1)}, bf16[8,1,16,1280]{3,2,1,0:T(8,128)(2,1)S(1)}, u32[]{:S(2)}, u32[]{:S(2)}) collective-permute-start(bf16[8,1,16,1280]{3,2,1,0:T(8,128)(2,1)S(1)} %all-to-all-done), channel_id=1, source_target_pairs={{0,8},{8,16},{16,24},{1,9},{9,17},{17,25},{2,10},{10,18},{18,26},{... | collective-permute-start | bytes 983048 | tf_op jit(solution)/shard_map/while/body/eval_jaxpr/ppermute | solution.py:25
  205.7 321.6 %while.40 = (s32[]{:T(128)}, bf16[8,1,16,1280]{3,2,1,0:T(8,128)(2,1)}, f32[1280,1920]{1,0:T(8,128)}, f32[1280,640]{1,0:T(8,128)}, s32[]{:T(128)}, /*index=5*/s32...) while((s32[]{:T(128)}, ...), condition=%wide.region_31.32_spmd.clone, body=%wide.region_13.31_spmd.clone.sunk | while | flops 2492336128 | bytes 115228824 | solution.py:297
  218.0 8.6 %select_add_fusion.4 = f32[1280,1920]{1,0:T(8,128)} fusion(f32[1280,1920]{1,0:T(8,128)} %get-tuple-element.971, f32[1280,1920]{1,0:T(8,128)} %get-tuple-element.1043, pred[]{:T(512)S(6)} %compare.4), kind=kLoop, calls=%fused_computation.158.clone.1 | loop fusion | flops 4915200 | bytes 29491200 | tf_op jit(solution)/shard_map/while/body/eval_jaxpr/add | solution.py:278
  252.8 11.4 %select_add_fusion.4 = f32[1280,1920]{1,0:T(8,128)} fusion(f32[1280,1920]{1,0:T(8,128)} %get-tuple-element.971, f32[1280,1920]{1,0:T(8,128)} %get-tuple-element.1043, pred[]{:T(512)S(6)} %compare.4), kind=kLoop, calls=%fused_computation.158.clone.1 | loop fusion | flops 4915200 | bytes 29491200 | tf_op jit(solution)/shard_map/while/body/eval_jaxpr/add | solution.py:278
  270.4 11.4 %collective-permute-done.1 = bf16[8,1,16,1280]{3,2,1,0:T(8,128)(2,1)S(1)} collective-permute-done((bf16[8,1,16,1280]{3,2,1,0:T(8,128)(2,1)S(1)}, bf16[8,1,16,1280]{3,2,1,0:T(8,128)(2,1)S(1)}, u32[]{:S(2)}, u32[]{:S(2)}) %collective-permute-start.1) | collective-permute-done | bytes 327712 | tf_op jit(solution)/shard_map/while/body/eval_jaxpr/ppermute | solution.py:25
  298.7 11.4 %select_add_fusion.4 = f32[1280,1920]{1,0:T(8,128)} fusion(f32[1280,1920]{1,0:T(8,128)} %get-tuple-element.971, f32[1280,1920]{1,0:T(8,128)} %get-tuple-element.1043, pred[]{:T(512)S(6)} %compare.4), kind=kLoop, calls=%fused_computation.158.clone.1 | loop fusion | flops 4915200 | bytes 29491200 | tf_op jit(solution)/shard_map/while/body/eval_jaxpr/add | solution.py:278
  316.3 78.5 %collective-permute-done.1 = bf16[8,1,16,1280]{3,2,1,0:T(8,128)(2,1)S(1)} collective-permute-done((bf16[8,1,16,1280]{3,2,1,0:T(8,128)(2,1)S(1)}, bf16[8,1,16,1280]{3,2,1,0:T(8,128)(2,1)S(1)}, u32[]{:S(2)}, u32[]{:S(2)}) %collective-permute-start.1) | collective-permute-done | bytes 327712 | tf_op jit(solution)/shard_map/while/body/eval_jaxpr/ppermute | solution.py:25
  395.5 35.9 %conditional.6 = (bf16[8,1,16,1280]{3,0,2,1:T(8,128)(2,1)}, f32[1280,1920]{1,0:T(8,128)}, f32[1280,640]{1,0:T(8,128)}) conditional(s32[]{:T(128)} %clamp.22, () %tuple.149, (pred[]{:T(512)}, s32[]{:T(128)}, bf16[2,8,1,16,1280]{4,1,3,2,0:T(8,128)(2,1)}, bf16[8,1,16,1280]{3,2,1,0:T(8,128)(2,1)}, ...), branch_computations={%region_14.14_spmd, %region_15.22_spmd, %region_23.30_spmd} | conditional | flops 2485782528 | bytes 71647032 | solution.py:275
  433.2 7.2 all-to-all-start.1
  440.4 11.4 %select_add_fusion.4 = f32[1280,1920]{1,0:T(8,128)} fusion(f32[1280,1920]{1,0:T(8,128)} %get-tuple-element.971, f32[1280,1920]{1,0:T(8,128)} %get-tuple-element.1043, pred[]{:T(512)S(6)} %compare.4), kind=kLoop, calls=%fused_computation.158.clone.1 | loop fusion | flops 4915200 | bytes 29491200 | tf_op jit(solution)/shard_map/while/body/eval_jaxpr/add | solution.py:278
  461.4 35.9 %conditional.6 = (bf16[8,1,16,1280]{3,0,2,1:T(8,128)(2,1)}, f32[1280,1920]{1,0:T(8,128)}, f32[1280,640]{1,0:T(8,128)}) conditional(s32[]{:T(128)} %clamp.22, () %tuple.149, (pred[]{:T(512)}, s32[]{:T(128)}, bf16[2,8,1,16,1280]{4,1,3,2,0:T(8,128)(2,1)}, bf16[8,1,16,1280]{3,2,1,0:T(8,128)(2,1)}, ...), branch_computations={%region_14.14_spmd, %region_15.22_spmd, %region_23.30_spmd} | conditional | flops 2485782528 | bytes 71647032 | solution.py:275
  499.1 7.2 all-to-all-start.1
  506.3 11.4 %select_add_fusion.4 = f32[1280,1920]{1,0:T(8,128)} fusion(f32[1280,1920]{1,0:T(8,128)} %get-tuple-element.971, f32[1280,1920]{1,0:T(8,128)} %get-tuple-element.1043, pred[]{:T(512)S(6)} %compare.4), kind=kLoop, calls=%fused_computation.158.clone.1 | loop fusion | flops 4915200 | bytes 29491200 | tf_op jit(solution)/shard_map/while/body/eval_jaxpr/add | solution.py:278
  529.2 214.1 %all-reduce.5.cloned.1.call-done = (f32[1280,1920]{1,0:T(8,128)}, f32[1280,640]{1,0:T(8,128)}) async-done(((f32[1280,1920]{1,0:T(8,128)}, f32[1280,640]{1,0:T(8,128)}), (f32[1280,1920]{1,0:T(8,128)}, f32[1280,640]{1,0:T(8,128)})) %all-reduce.5.cloned.1.call-update) | async-done | bytes 13107216
  (245 shorter events, 290.7 us)
Async XLA Ops:
  7.2 736.2 %all-reduce.5.cloned.1.call-start = ((), (), s32[]{:S(2)}) async-start(), calls=%async_computation.2 | async-start | bytes 26214400
  30.3 21.7 %all-to-all-start = ((bf16[8,1,16,1280]{3,2,1,0:T(8,128)(2,1)}), bf16[8,1,16,1280]{3,2,1,0:T(8,128)(2,1)S(1)}, u32[]{:S(2)}, u32[]{:S(2)}) async-start(bf16[8,1,16,1280]{3,2,1,0:T(8,128)(2,1)} %get-tuple-element.957), calls=%async_computation | async-start | bytes 655360 | tf_op jit(solution)/shard_map/while/body/eval_jaxpr/all_to_all | solution.py:211
  52.0 6.9 collective-permute-start
  66.1 10.5 %copy-start = (bf16[640,1280]{1,0:T(8,128)(2,1)S(1)}, bf16[640,1280]{1,0:T(8,128)(2,1)}, u32[]{:S(2)}) copy-start(bf16[640,1280]{1,0:T(8,128)(2,1)} %get-tuple-element.579) | copy-start | bytes 4915204 | tf_op jit(solution)/shard_map/while/body/eval_jaxpr/cond
  78.8 14.8 %all-to-all-start = ((bf16[8,1,16,1280]{3,2,1,0:T(8,128)(2,1)}), bf16[8,1,16,1280]{3,2,1,0:T(8,128)(2,1)S(1)}, u32[]{:S(2)}, u32[]{:S(2)}) async-start(bf16[8,1,16,1280]{3,2,1,0:T(8,128)(2,1)} %get-tuple-element.957), calls=%async_computation | async-start | bytes 655360 | tf_op jit(solution)/shard_map/while/body/eval_jaxpr/all_to_all | solution.py:211
  93.6 5.9 collective-permute-start
  101.3 14.5 %all-to-all-start = ((bf16[8,1,16,1280]{3,2,1,0:T(8,128)(2,1)}), bf16[8,1,16,1280]{3,2,1,0:T(8,128)(2,1)S(1)}, u32[]{:S(2)}, u32[]{:S(2)}) async-start(bf16[8,1,16,1280]{3,2,1,0:T(8,128)(2,1)} %get-tuple-element.957), calls=%async_computation | async-start | bytes 655360 | tf_op jit(solution)/shard_map/while/body/eval_jaxpr/all_to_all | solution.py:211
  115.9 19.7 %collective-permute-start = (bf16[8,1,16,1280]{3,2,1,0:T(8,128)(2,1)S(1)}, bf16[8,1,16,1280]{3,2,1,0:T(8,128)(2,1)S(1)}, u32[]{:S(2)}, u32[]{:S(2)}) collective-permute-start(bf16[8,1,16,1280]{3,2,1,0:T(8,128)(2,1)S(1)} %all-to-all-done), channel_id=1, source_target_pairs={{0,8},{8,16},{16,24},{1,9},{9,17},{17,25},{2,10},{10,18},{18,26},{... | collective-permute-start | bytes 983048 | tf_op jit(solution)/shard_map/while/body/eval_jaxpr/ppermute | solution.py:25
  137.5 14.5 %all-to-all-start = ((bf16[8,1,16,1280]{3,2,1,0:T(8,128)(2,1)}), bf16[8,1,16,1280]{3,2,1,0:T(8,128)(2,1)S(1)}, u32[]{:S(2)}, u32[]{:S(2)}) async-start(bf16[8,1,16,1280]{3,2,1,0:T(8,128)(2,1)} %get-tuple-element.957), calls=%async_computation | async-start | bytes 655360 | tf_op jit(solution)/shard_map/while/body/eval_jaxpr/all_to_all | solution.py:211
  152.0 9.6 %collective-permute-start = (bf16[8,1,16,1280]{3,2,1,0:T(8,128)(2,1)S(1)}, bf16[8,1,16,1280]{3,2,1,0:T(8,128)(2,1)S(1)}, u32[]{:S(2)}, u32[]{:S(2)}) collective-permute-start(bf16[8,1,16,1280]{3,2,1,0:T(8,128)(2,1)S(1)} %all-to-all-done), channel_id=1, source_target_pairs={{0,8},{8,16},{16,24},{1,9},{9,17},{17,25},{2,10},{10,18},{18,26},{... | collective-permute-start | bytes 983048 | tf_op jit(solution)/shard_map/while/body/eval_jaxpr/ppermute | solution.py:25
  163.4 14.5 %all-to-all-start = ((bf16[8,1,16,1280]{3,2,1,0:T(8,128)(2,1)}), bf16[8,1,16,1280]{3,2,1,0:T(8,128)(2,1)S(1)}, u32[]{:S(2)}, u32[]{:S(2)}) async-start(bf16[8,1,16,1280]{3,2,1,0:T(8,128)(2,1)} %get-tuple-element.957), calls=%async_computation | async-start | bytes 655360 | tf_op jit(solution)/shard_map/while/body/eval_jaxpr/all_to_all | solution.py:211
  178.0 27.0 %collective-permute-start = (bf16[8,1,16,1280]{3,2,1,0:T(8,128)(2,1)S(1)}, bf16[8,1,16,1280]{3,2,1,0:T(8,128)(2,1)S(1)}, u32[]{:S(2)}, u32[]{:S(2)}) collective-permute-start(bf16[8,1,16,1280]{3,2,1,0:T(8,128)(2,1)S(1)} %all-to-all-done), channel_id=1, source_target_pairs={{0,8},{8,16},{16,24},{1,9},{9,17},{17,25},{2,10},{10,18},{18,26},{... | collective-permute-start | bytes 983048 | tf_op jit(solution)/shard_map/while/body/eval_jaxpr/ppermute | solution.py:25
  214.6 14.5 %all-to-all-start.1 = ((bf16[8,1,16,1280]{3,2,1,0:T(8,128)(2,1)}), bf16[8,1,16,1280]{3,2,1,0:T(8,128)(2,1)S(1)}, u32[]{:S(2)}, u32[]{:S(2)}) async-start(bf16[8,1,16,1280]{3,2,1,0:T(8,128)(2,1)} %copy.227), calls=%async_computation.1 | async-start | bytes 655360 | tf_op jit(solution)/shard_map/while/body/eval_jaxpr/all_to_all | solution.py:282
  229.1 9.4 %collective-permute-start.1 = (bf16[8,1,16,1280]{3,2,1,0:T(8,128)(2,1)S(1)}, bf16[8,1,16,1280]{3,2,1,0:T(8,128)(2,1)S(1)}, u32[]{:S(2)}, u32[]{:S(2)}) collective-permute-start(bf16[8,1,16,1280]{3,2,1,0:T(8,128)(2,1)S(1)} %all-to-all-done.1), channel_id=1, source_target_pairs={{8,0},{16,8},{24,16},{9,1},{17,9},{25,17},{10,2},{18,10},{26,18},{... | collective-permute-start | bytes 983048 | tf_op jit(solution)/shard_map/while/body/eval_jaxpr/ppermute | solution.py:25
  248.2 16.0 %all-to-all-start.1 = ((bf16[8,1,16,1280]{3,2,1,0:T(8,128)(2,1)}), bf16[8,1,16,1280]{3,2,1,0:T(8,128)(2,1)S(1)}, u32[]{:S(2)}, u32[]{:S(2)}) async-start(bf16[8,1,16,1280]{3,2,1,0:T(8,128)(2,1)} %copy.227), calls=%async_computation.1 | async-start | bytes 655360 | tf_op jit(solution)/shard_map/while/body/eval_jaxpr/all_to_all | solution.py:282
  264.1 17.7 %collective-permute-start.1 = (bf16[8,1,16,1280]{3,2,1,0:T(8,128)(2,1)S(1)}, bf16[8,1,16,1280]{3,2,1,0:T(8,128)(2,1)S(1)}, u32[]{:S(2)}, u32[]{:S(2)}) collective-permute-start(bf16[8,1,16,1280]{3,2,1,0:T(8,128)(2,1)S(1)} %all-to-all-done.1), channel_id=1, source_target_pairs={{8,0},{16,8},{24,16},{9,1},{17,9},{25,17},{10,2},{18,10},{26,18},{... | collective-permute-start | bytes 983048 | tf_op jit(solution)/shard_map/while/body/eval_jaxpr/ppermute | solution.py:25
  291.5 18.6 %all-to-all-start.1 = ((bf16[8,1,16,1280]{3,2,1,0:T(8,128)(2,1)}), bf16[8,1,16,1280]{3,2,1,0:T(8,128)(2,1)S(1)}, u32[]{:S(2)}, u32[]{:S(2)}) async-start(bf16[8,1,16,1280]{3,2,1,0:T(8,128)(2,1)} %copy.227), calls=%async_computation.1 | async-start | bytes 655360 | tf_op jit(solution)/shard_map/while/body/eval_jaxpr/all_to_all | solution.py:282
  310.0 84.8 %collective-permute-start.1 = (bf16[8,1,16,1280]{3,2,1,0:T(8,128)(2,1)S(1)}, bf16[8,1,16,1280]{3,2,1,0:T(8,128)(2,1)S(1)}, u32[]{:S(2)}, u32[]{:S(2)}) collective-permute-start(bf16[8,1,16,1280]{3,2,1,0:T(8,128)(2,1)S(1)} %all-to-all-done.1), channel_id=1, source_target_pairs={{8,0},{16,8},{24,16},{9,1},{17,9},{25,17},{10,2},{18,10},{26,18},{... | collective-permute-start | bytes 983048 | tf_op jit(solution)/shard_map/while/body/eval_jaxpr/ppermute | solution.py:25
  396.1 10.6 %copy-start.2 = (bf16[640,1280]{1,0:T(8,128)(2,1)S(1)}, bf16[640,1280]{1,0:T(8,128)(2,1)}, u32[]{:S(2)}) copy-start(bf16[640,1280]{1,0:T(8,128)(2,1)} %get-tuple-element.601) | copy-start | bytes 4915204 | tf_op jit(solution)/shard_map/while/body/eval_jaxpr/cond
  433.2 18.6 %all-to-all-start.1 = ((bf16[8,1,16,1280]{3,2,1,0:T(8,128)(2,1)}), bf16[8,1,16,1280]{3,2,1,0:T(8,128)(2,1)S(1)}, u32[]{:S(2)}, u32[]{:S(2)}) async-start(bf16[8,1,16,1280]{3,2,1,0:T(8,128)(2,1)} %copy.227), calls=%async_computation.1 | async-start | bytes 655360 | tf_op jit(solution)/shard_map/while/body/eval_jaxpr/all_to_all | solution.py:282
  451.7 9.0 %collective-permute-start.1 = (bf16[8,1,16,1280]{3,2,1,0:T(8,128)(2,1)S(1)}, bf16[8,1,16,1280]{3,2,1,0:T(8,128)(2,1)S(1)}, u32[]{:S(2)}, u32[]{:S(2)}) collective-permute-start(bf16[8,1,16,1280]{3,2,1,0:T(8,128)(2,1)S(1)} %all-to-all-done.1), channel_id=1, source_target_pairs={{8,0},{16,8},{24,16},{9,1},{17,9},{25,17},{10,2},{18,10},{26,18},{... | collective-permute-start | bytes 983048 | tf_op jit(solution)/shard_map/while/body/eval_jaxpr/ppermute | solution.py:25
  462.0 10.6 %copy-start.2 = (bf16[640,1280]{1,0:T(8,128)(2,1)S(1)}, bf16[640,1280]{1,0:T(8,128)(2,1)}, u32[]{:S(2)}) copy-start(bf16[640,1280]{1,0:T(8,128)(2,1)} %get-tuple-element.601) | copy-start | bytes 4915204 | tf_op jit(solution)/shard_map/while/body/eval_jaxpr/cond
  499.1 18.6 %all-to-all-start.1 = ((bf16[8,1,16,1280]{3,2,1,0:T(8,128)(2,1)}), bf16[8,1,16,1280]{3,2,1,0:T(8,128)(2,1)S(1)}, u32[]{:S(2)}, u32[]{:S(2)}) async-start(bf16[8,1,16,1280]{3,2,1,0:T(8,128)(2,1)} %copy.227), calls=%async_computation.1 | async-start | bytes 655360 | tf_op jit(solution)/shard_map/while/body/eval_jaxpr/all_to_all | solution.py:282
  517.6 9.0 %collective-permute-start.1 = (bf16[8,1,16,1280]{3,2,1,0:T(8,128)(2,1)S(1)}, bf16[8,1,16,1280]{3,2,1,0:T(8,128)(2,1)S(1)}, u32[]{:S(2)}, u32[]{:S(2)}) collective-permute-start(bf16[8,1,16,1280]{3,2,1,0:T(8,128)(2,1)S(1)} %all-to-all-done.1), channel_id=1, source_target_pairs={{8,0},{16,8},{24,16},{9,1},{17,9},{25,17},{10,2},{18,10},{26,18},{... | collective-permute-start | bytes 983048 | tf_op jit(solution)/shard_map/while/body/eval_jaxpr/ppermute | solution.py:25
  (17 other events, 86.9 us)
Sparse Core Ops, SparseCore 0:
  527.5 215.8 all-reduce.4
where the time goes:
time: 757 us; the launch traced here: 754 us
  waiting for transfers between devices  388 us (51%)
  starting transfers between devices  104 us (14%)
  other arithmetic  96.1 us (13%)
  local copies, waits for them, and re-layouts  75.9 us (10%)
  matrix products  74.6 us (10%)
  between operations  14.7 us (2%)
    unnamed x2, waiting for transfers between devices  214 us
    ppermute x10, waiting for transfers between devices, shifted(): return lax.ppermute(x, axis, pairs)  119 us
    add x5, other arithmetic, backward_tick(): total_qkv = total_qkv + grad_qkv_term  54 us
    all_to_all x5, waiting for transfers between devices, forward_tick(): lax.all_to_all(shortened(result), 'seq', split_axis=0, concat_axis=0, til...  52.3 us
    ppermute x10, starting transfers between devices, shifted(): return lax.ppermute(x, axis, pairs)  51.6 us
    all_to_all x5, starting transfers between devices, backward_tick(): lax.all_to_all(shortened(back_block), 'seq', split_axis=0, concat_axis=0,...  29.7 us
    another operation x16, local copies, waits for them, and re-layouts  25.3 us
    add x5, other arithmetic, backward_tick(): total_out = total_out + grad_out_term  24 us
  transfers between devices with their start and end apart: 21, of which 17 were waited for; matrix products, arithmetic and copies ran while one was open for 12% of the time, Pallas kernels for 0%

commit v1 on v0

v1 whole, which is shorter than its diff:
```python
import functools
import math

import jax
import jax.numpy as jnp
from jax import lax
from jax.experimental import pallas as pl
from jax.experimental.pallas import tpu as pltpu
from jax.sharding import PartitionSpec as P

HEAD_DIM = 64
NORM_EPS = 1e-05
MASKED = -1e30
MESH = pl.DeviceIdType.MESH


def dot(a, b, a_dim, b_dim):
    return lax.dot_general(
        a, b, (((a_dim,), (b_dim,)), ((), ())), preferred_element_type=jnp.float32
    )


def relay_kernel(
    seq_count,
    section_count,
    x_hbm,
    w_qkv_hbm,
    w_out_hbm,
    g_hbm,
    out_hbm,
    grad_qkv_ref,
    grad_out_ref,
    wq,
    wo,
    xb,
    gb,
    ub,
    rb,
    nb,
    pk,
    pr,
    mx,
    dpk,
    hb,
    bb,
    in_sem,
    x_send,
    x_recv,
    g_send,
    g_recv,
    o_send,
    o_recv,
):
    dp_id = lax.axis_index("dp")
    section = lax.axis_index("section")
    seq_id = lax.axis_index("seq")
    micro_count, rows, width = xb.shape
    block = rows // seq_count
    inner = wo.shape[0]
    pairs = inner // (2 * HEAD_DIM)
    scale = 1.0 / math.sqrt(HEAD_DIM)
    is_first = section == 0
    is_last = section == section_count - 1
    is_odd = lax.rem(section, 2) == 1

    load_wq = pltpu.make_async_copy(w_qkv_hbm, wq, in_sem.at[0])
    load_wo = pltpu.make_async_copy(w_out_hbm, wo, in_sem.at[1])
    load_x = pltpu.make_async_copy(x_hbm, xb, in_sem.at[2])
    load_g = pltpu.make_async_copy(g_hbm, gb, in_sem.at[3])

    @pl.when(is_first)
    def _():
        load_x.start()

    load_wq.start()
    load_wo.start()

    @pl.when(is_last)
    def _():
        load_g.start()

    barrier = pltpu.get_barrier_semaphore()

    @pl.when(section > 0)
    def _():
        for k in range(seq_count):
            pl.semaphore_signal(
                barrier, inc=1, device_id=(dp_id, section - 1, k), device_id_type=MESH
            )

    @pl.when(section < section_count - 1)
    def _():
        for k in range(seq_count):
            pl.semaphore_signal(
                barrier, inc=1, device_id=(dp_id, section + 1, k), device_id_type=MESH
            )

    inner_section = jnp.logical_and(section > 0, section < section_count - 1)
    pl.semaphore_wait(barrier, jnp.where(inner_section, 2 * seq_count, seq_count))

    def hop(src, dst, send, recv, m, k, step):
        return pltpu.make_async_remote_copy(
            src_ref=src.at[m, pl.ds(k * block, block), :],
            dst_ref=dst.at[m, pl.ds(seq_id * block, block), :],
            send_sem=send.at[m, k],
            recv_sem=recv.at[m, seq_id],
            device_id=(dp_id, section + step, k),
            device_id_type=MESH,
        )

    def arrival(dst, recv, m, k):
        landed = dst.at[m, pl.ds(k * block, block), :]
        return pltpu.make_async_copy(landed, landed, recv.at[m, k])

    def output_back(m):
        return pltpu.make_async_remote_copy(
            src_ref=xb.at[m],
            dst_ref=out_hbm.at[m],
            send_sem=o_send.at[m],
            recv_sem=o_recv.at[m],
            device_id=(dp_id, section - 1, seq_id),
            device_id_type=MESH,
        )

    def output_own(m):
        return pltpu.make_async_copy(hb.at[m], out_hbm.at[m], o_recv.at[m])

    lane = lax.broadcasted_iota(jnp.int32, (rows, 2 * HEAD_DIM), 1)
    first_head = lane < HEAD_DIM
    row_group = lax.rem(lax.broadcasted_iota(jnp.int32, (2 * rows, rows), 0), block)
    col_group = lax.rem(lax.broadcasted_iota(jnp.int32, (2 * rows, rows), 1), block)
    same_group = jnp.where(row_group == col_group, 1, 0) + jnp.where(is_odd, 1, 0) > 0

    def stacked(part):
        zero = jnp.zeros_like(part)
        return jnp.concatenate(
            [jnp.where(first_head, part, zero), jnp.where(first_head, zero, part)], axis=0
        )

    def joined(part):
        return jnp.where(first_head, part[:rows], part[rows:])

    def forward(m, carry):
        @pl.when(section > 0)
        def _():
            for k in range(seq_count):
                arrival(xb, x_recv, m, k).wait()

        @pl.when(is_odd)
        def _():
            output_back(m).start()

        values = xb[m].astype(jnp.float32)
        centred = values - jnp.mean(values, axis=-1, keepdims=True)
        inverse = lax.rsqrt(jnp.mean(centred * centred, axis=-1, keepdims=True) + NORM_EPS)
        unit = centred * inverse
        ub[m] = unit
        rb[m] = jnp.broadcast_to(inverse, (rows, 128))
        nb[m] = unit.astype(jnp.bfloat16)
        pk[m] = dot(nb[m], wq[...], 1, 0).astype(jnp.bfloat16)
        for p in range(pairs):
            cols = pl.ds(p * 128, 128)
            query = pk[m, :, pl.ds(p * 128, 128)]
            key = pk[m, :, pl.ds(inner + p * 128, 128)]
            value = pk[m, :, pl.ds(2 * inner + p * 128, 128)]
            scores = dot(stacked(query), key, 1, 1) * scale
            scores = jnp.where(same_group, scores, MASKED)
            exps = jnp.exp(scores - jnp.max(scores, axis=-1, keepdims=True))
            probs = exps / jnp.sum(exps, axis=-1, keepdims=True)
            pr[m, p] = probs
            mx[m, :, cols] = joined(dot(probs.astype(jnp.bfloat16), value, 1, 0)).astype(
                jnp.bfloat16
            )
        hb[m] = (xb[m].astype(jnp.float32) + dot(mx[m], wo[...], 1, 0)).astype(jnp.bfloat16)

        @pl.when(section < section_count - 1)
        def _():
            for k in range(seq_count):
                hop(hb, xb, x_send, x_recv, m, k, 1).start()

        @pl.when(is_odd)
        def _():
            output_own(m).start()

        return carry

    def backward(m, carry):
        @pl.when(section < section_count - 1)
        def _():
            for k in range(seq_count):
                arrival(gb, g_recv, m, k).wait()

        d_mixed = dot(gb[m], wo[...], 1, 1).astype(jnp.bfloat16)
        for p in range(pairs):
            query = stacked(pk[m, :, pl.ds(p * 128, 128)])
            key = pk[m, :, pl.ds(inner + p * 128, 128)]
            value = pk[m, :, pl.ds(2 * inner + p * 128, 128)]
            d_heads = stacked(d_mixed[:, p * 128 : (p + 1) * 128])
            probs = pr[m, p]
            d_values = dot(probs.astype(jnp.bfloat16), d_heads, 0, 0)
            d_probs = dot(d_heads, value, 1, 1)
            d_scores = probs * (d_probs - jnp.sum(probs * d_probs, axis=-1, keepdims=True))
            d_scores = d_scores.astype(jnp.bfloat16)
            d_query = joined(dot(d_scores, key, 1, 0)) * scale
            d_keys = dot(d_scores, query, 0, 0) * scale
            dpk[m, :, pl.ds(p * 128, 128)] = d_query.astype(jnp.bfloat16)
            dpk[m, :, pl.ds(inner + p * 128, 128)] = d_keys.astype(jnp.bfloat16)
            dpk[m, :, pl.ds(2 * inner + p * 128, 128)] = d_values.astype(jnp.bfloat16)

        @pl.when(section > 0)
        def _():
            d_normed = dot(dpk[m], wq[...], 1, 1)
            unit = ub[m]
            d_inside = rb[m, :, 0:1] * (
                d_normed
                - jnp.mean(d_normed, axis=-1, keepdims=True)
                - unit * jnp.mean(d_normed * unit, axis=-1, keepdims=True)
            )
            bb[m] = (gb[m].astype(jnp.float32) + d_inside).astype(jnp.bfloat16)
            for k in range(seq_count):
                hop(bb, gb, g_send, g_recv, m, k, -1).start()

        return carry

    @pl.when(is_first)
    def _():
        load_x.wait()

    load_wq.wait()
    load_wo.wait()
    lax.fori_loop(0, micro_count, forward, 0)

    @pl.when(is_last)
    def _():
        load_g.wait()

    lax.fori_loop(0, micro_count, backward, 0)

    chunk = 256 if width % 256 == 0 else 128

    def weight_grads(i, carry):
        cols = pl.ds(pl.multiple_of(i * chunk, chunk), chunk)
        normed = nb[:, :, cols].reshape(micro_count * rows, chunk)
        grads = gb[:, :, cols].reshape(micro_count * rows, chunk)
        d_packed = dpk[...].reshape(micro_count * rows, 3 * inner)
        mixed = mx[...].reshape(micro_count * rows, inner)
        grad_qkv_ref[cols, :] = dot(normed, d_packed, 0, 0).astype(jnp.bfloat16)
        grad_out_ref[cols, :] = dot(grads, mixed, 0, 0).astype(jnp.bfloat16)
        return carry

    lax.fori_loop(0, width // chunk, weight_grads, 0)

    for m in range(micro_count):

        @pl.when(section < section_count - 1)
        def _():
            for k in range(seq_count):
                hop(hb, xb, x_send, x_recv, m, k, 1).wait_send()

        @pl.when(section > 0)
        def _():
            for k in range(seq_count):
                hop(bb, gb, g_send, g_recv, m, k, -1).wait_send()

        @pl.when(is_odd)
        def _():
            output_back(m).wait_send()
            output_own(m).wait()

        @pl.when(jnp.logical_not(is_odd))
        def _():
            pltpu.make_async_copy(out_hbm.at[m], out_hbm.at[m], o_recv.at[m]).wait()


def relay(seq_count, section_count, x, w_qkv, w_out, g):
    micro_count, rows, width = x.shape
    inner = w_out.shape[0]
    pairs = inner // (2 * HEAD_DIM)
    bf16, f32 = jnp.bfloat16, jnp.float32
    tokens = (micro_count, rows, width)
    dma = pltpu.SemaphoreType.DMA
    any_spec = pl.BlockSpec(memory_space=pl.ANY)
    vmem_spec = pl.BlockSpec(memory_space=pltpu.VMEM)
    return pl.pallas_call(
        functools.partial(relay_kernel, seq_count, section_count),
        out_shape=(
            jax.ShapeDtypeStruct(tokens, bf16),
            jax.ShapeDtypeStruct((width, 3 * inner), bf16),
            jax.ShapeDtypeStruct((width, inner), bf16),
        ),
        in_specs=[any_spec] * 4,
        out_specs=(any_spec, vmem_spec, vmem_spec),
        scratch_shapes=[
            pltpu.VMEM((width, 3 * inner), bf16),
            pltpu.VMEM((inner, width), bf16),
            pltpu.VMEM(tokens, bf16),
            pltpu.VMEM(tokens, bf16),
            pltpu.VMEM(tokens, f32),
            pltpu.VMEM((micro_count, rows, 128), f32),
            pltpu.VMEM(tokens, bf16),
            pltpu.VMEM((micro_count, rows, 3 * inner), bf16),
            pltpu.VMEM((micro_count, pairs, 2 * rows, rows), f32),
            pltpu.VMEM((micro_count, rows, inner), bf16),
            pltpu.VMEM((micro_count, rows, 3 * inner), bf16),
            pltpu.VMEM(tokens, bf16),
            pltpu.VMEM(tokens, bf16),
            dma((4,)),
            dma((micro_count, seq_count)),
            dma((micro_count, seq_count)),
            dma((micro_count, seq_count)),
            dma((micro_count, seq_count)),
            dma((micro_count,)),
            dma((micro_count,)),
        ],
        compiler_params=pltpu.CompilerParams(
            collective_id=0, has_side_effects=True, vmem_limit_bytes=60 * 1024 * 1024
        ),
        name="relay",
    )(x, w_qkv, w_out, g)


def local(clips_in, w_qkv, w_out, out_cotangent):
    seq_count = lax.axis_size("seq")
    section_count = lax.axis_size("section")
    micro_count, frames, patches_dev, width = clips_in.shape
    x = clips_in.reshape(micro_count, frames * patches_dev, width)
    g = out_cotangent.reshape(micro_count, -1, width)
    outputs, grad_qkv, grad_out = relay(seq_count, section_count, x, w_qkv[0], w_out[0], g)
    shards = []
    for part in (grad_qkv, grad_out):
        group = lax.axis_size("dp") * seq_count
        blocks = part.reshape(group, part.shape[0] // group, part.shape[1])
        shard = lax.psum_scatter(blocks, ("dp", "seq"), scatter_dimension=0, tiled=False)
        shards.append(shard.astype(jnp.float32))
    return (
        outputs.reshape((1,) + out_cotangent.shape),
        shards[0][None],
        shards[1][None],
    )


def solution(mesh):
    return jax.shard_map(
        local,
        mesh=mesh,
        in_specs=(
            P("dp", None, "seq", None),
            P("section", None, None),
            P("section", None, None),
            P("dp", "seq", None, None),
        ),
        out_specs=(
            P("section", "dp", "seq", None, None),
            P("section", ("dp", "seq"), None),
            P("section", ("dp", "seq"), None),
        ),
        check_vma=False,
    )
```

time: 757 us -> 420 us (0.55)
  Pallas kernels: 0 us -> 112 us
  waiting for transfers between devices: 388 us -> 277 us
  starting transfers between devices: 104 us -> 0.08 us
  other arithmetic: 96.1 us -> 0 us
  matrix products: 74.6 us -> 0 us
  local copies, waits for them, and re-layouts: 75.9 us -> 14.9 us
    ppermute x10 -> x0, waiting for transfers between devices: 119 us -> none  [shifted(): return lax.ppermute(x, axis, pairs)]
    pallas_call x0 -> x1, Pallas kernels: none -> 112 us  [relay(): pl.pallas_call(functools.partial(relay_kernel, seq_count, section_count),...]
    add x10 -> x0, other arithmetic: 78 us -> none  [the longest x5 54 us: backward_tick(): total_qkv = total_qkv + grad_qkv_term]
    dot_general x28 -> x0, matrix products: 64.7 us -> none  [the longest x4 13.6 us: project(): jnp.dot(normed, weight_qkv, preferred_element_type=jnp.float32)]
    unnamed x2 -> x4, waiting for transfers between devices: 214 us -> 277 us
    all_to_all x10 -> x0, waiting for transfers between devices: 54.8 us -> none  [the longest x5 52.3 us: forward_tick(): lax.all_to_all(shortened(result), 'seq', split_axis=0, concat_axis=0, til...]
    all_to_all x10 -> x0, starting transfers between devices: 51.9 us -> none  [the longest x5 29.7 us: backward_tick(): lax.all_to_all(shortened(back_block), 'seq', split_axis=0, concat_axis=0,...]
    ppermute x10 -> x0, starting transfers between devices: 51.6 us -> none  [shifted(): return lax.ppermute(x, axis, pairs)]
  transfers between devices with their start and end apart: 21 -> 2, of which waited for: 17 -> 2; matrix products, arithmetic and copies ran while one was open for 12% -> 2% of each run, Pallas kernels for 0% -> 0%
where the time goes in v1:
time: 420 us; the launch traced here: 419 us
  waiting for transfers between devices  277 us (66%)
  Pallas kernels  112 us (27%)
  local copies, waits for them, and re-layouts  14.9 us (4%)
  between operations  14 us (3%)
    unnamed x4, waiting for transfers between devices  277 us
    pallas_call x1, Pallas kernels, relay(): pl.pallas_call(functools.partial(relay_kernel, seq_count, section_count),...  112 us
    reshape x2, local copies, waits for them, and re-layouts, local(): blocks = part.reshape(group, part.shape[0] // group, part.shape[1])  11 us
  transfers between devices with their start and end apart: 2, of which 2 were waited for; matrix products, arithmetic and copies ran while one was open for 2% of the time, Pallas kernels for 0%

profile of v1, /device:TPU:2, one launch (start us, length us, event | category | flops | bytes accessed | tf_op | source)
XLA Modules:
  0.0 418.9 jit_solution(13428507543513971937)
XLA Ops:
  7.2 0.0 reduce-scatter.9.cloned.1.call-start
  7.2 112.4 %relay.1 = (bf16[2,128,1280]{2,1,0:T(8,128)(2,1)}, bf16[1280,1920]{1,0:T(8,128)(2,1)}, bf16[1280,640]{1,0:T(8,128)(2,1)}) custom-call(bf16[2,128,1280]{2,1,0:T(8,128)(2,1)} %bitcast.11, bf16[1280,1920]{1,0:T(8,128)(2,1)} %bitcast.8, bf16[640,1280]{1,0:T(8,128)(2,1)} %bitcast.9, bf16[2,128,1280]{2,1,0:T(8,128)(2,1)} %bitcast.12), custom_call_target="tpu_custom_call" | custom-call | tf_op jit(solution)/shard_map/relay/pallas_call | solution.py:284
  119.6 3.6 reshape.25
  123.2 0.0 reduce-scatter.9.cloned.1.call-update
  123.2 0.0 reduce-scatter.7.cloned.1.call-start
  123.2 7.4 %reshape.24 = bf16[64,20,1920]{2,1,0:T(8,128)(2,1)} reshape(bf16[1280,1920]{1,0:T(8,128)(2,1)} %get-tuple-element.7) | data formatting | bytes 9830400 | tf_op jit(solution)/shard_map/reshape | solution.py:332
  130.6 0.0 copy-start
  130.6 0.0 reduce-scatter.7.cloned.1.call-update
  130.6 130.5 %reduce-scatter.9.cloned.1.call-done = bf16[1,20,640]{2,1,0:T(8,128)(2,1)} async-done(((bf16[64,20,640]{2,1,0:T(8,128)(2,1)}), bf16[1,20,640]{2,1,0:T(8,128)(2,1)}) %reduce-scatter.9.cloned.1.call-update) | async-done | bytes 25616
  261.2 1.4 copy.15
  262.6 146.9 %reduce-scatter.7.cloned.1.call-done = bf16[1,20,1920]{2,1,0:T(8,128)(2,1)} async-done(((bf16[64,20,1920]{2,1,0:T(8,128)(2,1)}), bf16[1,20,1920]{2,1,0:T(8,128)(2,1)}) %reduce-scatter.7.cloned.1.call-update) | async-done | bytes 76816
  409.5 1.7 copy.14
  411.2 0.0 copy-done
  411.2 0.8 copy.17
Async XLA Ops:
  7.2 254.0 %reduce-scatter.9.cloned.1.call-start = ((), (), s32[]{:S(2)}) async-start(), calls=%async_computation.3 | async-start | bytes 1996800
  123.2 286.3 %reduce-scatter.7.cloned.1.call-start = ((), (), s32[]{:S(2)}) async-start(), calls=%async_computation.2 | async-start | bytes 5990400
  130.6 280.6 %copy-start = (bf16[2,128,1280]{2,1,0:T(8,128)(2,1)S(1)}, bf16[2,128,1280]{2,1,0:T(8,128)(2,1)}, u32[]{:S(2)}) copy-start(bf16[2,128,1280]{2,1,0:T(8,128)(2,1)} %get-tuple-element.6) | copy-start | bytes 1966084
Sparse Core Ops, SparseCore 0:
  123.3 137.8 reduce-scatter.8
  265.5 143.9 reduce-scatter.6

commit v2 on v1

--- a/solution.py
+++ b/solution.py
@@ -50,6 +50,19 @@
     g_recv,
     o_send,
     o_recv,
+    cw,
+    core_in,
+    xs,
+    x_in,
+    block_sum,
+    zs,
+    z_in,
+    core_send,
+    core_recv,
+    ring_x_send,
+    ring_x_recv,
+    ring_z_send,
+    ring_z_recv,
 ):
     dp_id = lax.axis_index("dp")
     section = lax.axis_index("section")
@@ -59,6 +72,10 @@
     inner = wo.shape[0]
     pairs = inner // (2 * HEAD_DIM)
     scale = 1.0 / math.sqrt(HEAD_DIM)
+    dp_count = lax.axis_size("dp")
+    x_count = dp_count // 2
+    x_id = dp_id // 2
+    core = lax.rem(dp_id, 2)
     is_first = section == 0
     is_last = section == section_count - 1
     is_odd = lax.rem(section, 2) == 1
@@ -95,8 +112,17 @@
                 barrier, inc=1, device_id=(dp_id, section + 1, k), device_id_type=MESH
             )
 
+    def at_x(step):
+        return (2 * lax.rem(x_id + step + x_count, x_count) + core, section, seq_id)
+
+    def at_z(step):
+        return (dp_id, section, lax.rem(seq_id + step + seq_count, seq_count))
+
+    other_core = (2 * x_id + 1 - core, section, seq_id)
+    for peer in (other_core, at_x(1), at_x(-1), at_z(1), at_z(-1)):
+        pl.semaphore_signal(barrier, inc=1, device_id=peer, device_id_type=MESH)
     inner_section = jnp.logical_and(section > 0, section < section_count - 1)
-    pl.semaphore_wait(barrier, jnp.where(inner_section, 2 * seq_count, seq_count))
+    pl.semaphore_wait(barrier, jnp.where(inner_section, 2 * seq_count + 5, seq_count + 5))
 
     def hop(src, dst, send, recv, m, k, step):
         return pltpu.make_async_remote_copy(
@@ -236,19 +262,140 @@
 
     lax.fori_loop(0, micro_count, backward, 0)
 
-    chunk = 256 if width % 256 == 0 else 128
-
-    def weight_grads(i, carry):
-        cols = pl.ds(pl.multiple_of(i * chunk, chunk), chunk)
-        normed = nb[:, :, cols].reshape(micro_count * rows, chunk)
-        grads = gb[:, :, cols].reshape(micro_count * rows, chunk)
-        d_packed = dpk[...].reshape(micro_count * rows, 3 * inner)
-        mixed = mx[...].reshape(micro_count * rows, inner)
-        grad_qkv_ref[cols, :] = dot(normed, d_packed, 0, 0).astype(jnp.bfloat16)
-        grad_out_ref[cols, :] = dot(grads, mixed, 0, 0).astype(jnp.bfloat16)
-        return carry
-
-    lax.fori_loop(0, width // chunk, weight_grads, 0)
+    tile = 256 if width % 256 == 0 else 128
+    tokens = micro_count * rows
+    dp_rows = width // dp_count
+    own_rows = dp_rows // seq_count
+    chunks = 4
+
+    def partial_grads(c):
+        if c < 3:
+            right = dpk[:, :, c * inner : (c + 1) * inner].reshape(tokens, inner)
+            left_ref = nb
+        else:
+            right = mx[...].reshape(tokens, inner)
+            left_ref = gb
+
+        def rows_of(i, carry):
+            cols = pl.ds(pl.multiple_of(i * tile, tile), tile)
+            left = left_ref[:, :, cols].reshape(tokens, tile)
+            cw[c, cols, :] = dot(left, right, 0, 0).astype(jnp.bfloat16)
+            return carry
+
+        lax.fori_loop(0, width // tile, rows_of, 0)
+
+    def block_rows(x, of_core):
+        return pl.ds(pl.multiple_of((2 * x + of_core) * dp_rows, dp_rows), dp_rows)
+
+    def core_copy(c, x):
+        return pltpu.make_async_remote_copy(
+            src_ref=cw.at[c, block_rows(x, 1 - core), :],
+            dst_ref=core_in.at[c, x],
+            send_sem=core_send.at[c, x],
+            recv_sem=core_recv.at[c, x],
+            device_id=other_core,
+            device_id_type=MESH,
+        )
+
+    def reach(count, c, way):
+        return count // 2 if (c + way) % 2 == 0 else count // 2 - 1
+
+    def ring_copy(own, landing, send, recv, c, way, distance, count, me, at):
+        step = 1 if way == 0 else -1
+        target = lax.rem(me + step * distance + count, count)
+        return pltpu.make_async_remote_copy(
+            src_ref=own.at[c, target],
+            dst_ref=landing.at[c, way, distance - 1],
+            send_sem=send.at[c, way, distance - 1],
+            recv_sem=recv.at[c, way, distance - 1],
+            device_id=at(step),
+            device_id_type=MESH,
+        )
+
+    def x_copy(c, way, distance):
+        return ring_copy(
+            xs, x_in, ring_x_send, ring_x_recv, c, way, distance, x_count, x_id, at_x
+        )
+
+    def z_copy(c, way, distance):
+        return ring_copy(
+            zs, z_in, ring_z_send, ring_z_recv, c, way, distance, seq_count, seq_id, at_z
+        )
+
+    def ring_step(copy, own, landing, count, me, c, distance):
+        for way in range(2):
+            limit = reach(count, c, way)
+            if distance > limit:
+                continue
+            if distance < limit:
+                copy(c, way, distance + 1).wait_recv()
+                step = 1 if way == 0 else -1
+                target = lax.rem(me + step * distance + count, count)
+                own[c, target] = (
+                    own[c, target].astype(jnp.float32)
+                    + landing[c, way, distance].astype(jnp.float32)
+                ).astype(jnp.bfloat16)
+            copy(c, way, distance).start()
+
+    def ring_total(copy, own, landing, count, me, c):
+        total = own[c, me].astype(jnp.float32)
+        for way in range(2):
+            if reach(count, c, way) > 0:
+                copy(c, way, 1).wait_recv()
+                total = total + landing[c, way, 0].astype(jnp.float32)
+        return total
+
+    def start_core(c):
+        partial_grads(c)
+        for x in range(x_count):
+            core_copy(c, x).start()
+
+    def start_x(c):
+        for x in range(x_count):
+            core_copy(c, x).wait_recv()
+            xs[c, x] = (
+                cw[c, block_rows(x, core), :].astype(jnp.float32)
+                + core_in[c, x].astype(jnp.float32)
+            ).astype(jnp.bfloat16)
+        ring_step(x_copy, xs, x_in, x_count, x_id, c, x_count // 2)
+
+    def next_x(c, distance):
+        ring_step(x_copy, xs, x_in, x_count, x_id, c, distance)
+
+    def start_z(c):
+        block_sum[...] = ring_total(x_copy, xs, x_in, x_count, x_id, c)
+        for k in range(seq_count):
+            zs[c, k] = block_sum[k * own_rows : (k + 1) * own_rows, :].astype(jnp.bfloat16)
+        ring_step(z_copy, zs, z_in, seq_count, seq_id, c, seq_count // 2)
+
+    def next_z(c, distance):
+        ring_step(z_copy, zs, z_in, seq_count, seq_id, c, distance)
+
+    def finish(c):
+        total = ring_total(z_copy, zs, z_in, seq_count, seq_id, c)
+        if c < 3:
+            grad_qkv_ref[:, c * inner : (c + 1) * inner] = total
+        else:
+            grad_out_ref[...] = total
+
+    stages = [start_core, start_x]
+    stages += [functools.partial(next_x, distance=d) for d in range(x_count // 2 - 1, 0, -1)]
+    stages += [start_z]
+    stages += [functools.partial(next_z, distance=d) for d in range(seq_count // 2 - 1, 0, -1)]
+    stages += [finish]
+    for tick in range(chunks + len(stages) - 1):
+        for c in range(chunks):
+            if 0 <= tick - c < len(stages):
+                stages[tick - c](c)
+
+    for c in range(chunks):
+        for x in range(x_count):
+            core_copy(c, x).wait_send()
+        for way in range(2):
+            for d in range(1, reach(x_count, c, way) + 1):
+                x_copy(c, way, d).wait_send()
+            for d in range(1, reach(seq_count, c, way) + 1):
+                z_copy(c, way, d).wait_send()
 
     for m in range(micro_count):
 
@@ -279,14 +426,18 @@
     bf16, f32 = jnp.bfloat16, jnp.float32
     tokens = (micro_count, rows, width)
     dma = pltpu.SemaphoreType.DMA
+    dp_count = lax.axis_size("dp")
+    x_count = dp_count // 2
+    dp_rows = width // dp_count
+    own_rows = dp_rows // seq_count
     any_spec = pl.BlockSpec(memory_space=pl.ANY)
     vmem_spec = pl.BlockSpec(memory_space=pltpu.VMEM)
     return pl.pallas_call(
         functools.partial(relay_kernel, seq_count, section_count),
         out_shape=(
             jax.ShapeDtypeStruct(tokens, bf16),
-            jax.ShapeDtypeStruct((width, 3 * inner), bf16),
-            jax.ShapeDtypeStruct((width, inner), bf16),
+            jax.ShapeDtypeStruct((own_rows, 3 * inner), f32),
+            jax.ShapeDtypeStruct((own_rows, inner), f32),
         ),
         in_specs=[any_spec] * 4,
         out_specs=(any_spec, vmem_spec, vmem_spec),
@@ -311,6 +462,19 @@
             dma((micro_count, seq_count)),
             dma((micro_count,)),
             dma((micro_count,)),
+            pltpu.VMEM((4, width, inner), bf16),
+            pltpu.VMEM((4, x_count, dp_rows, inner), bf16),
+            pltpu.VMEM((4, x_count, dp_rows, inner), bf16),
+            pltpu.VMEM((4, 2, x_count // 2, dp_rows, inner), bf16),
+            pltpu.VMEM((dp_rows, inner), f32),
+            pltpu.VMEM((4, seq_count, own_rows, inner), bf16),
+            pltpu.VMEM((4, 2, seq_count // 2, own_rows, inner), bf16),
+            dma((4, x_count)),
+            dma((4, x_count)),
+            dma((4, 2, x_count // 2)),
+            dma((4, 2, x_count // 2)),
+            dma((4, 2, seq_count // 2)),
+            dma((4, 2, seq_count // 2)),
         ],
         compiler_params=pltpu.CompilerParams(
             collective_id=0, has_side_effects=True, vmem_limit_bytes=60 * 1024 * 1024
@@ -326,17 +490,7 @@
     x = clips_in.reshape(micro_count, frames * patches_dev, width)
     g = out_cotangent.reshape(micro_count, -1, width)
     outputs, grad_qkv, grad_out = relay(seq_count, section_count, x, w_qkv[0], w_out[0], g)
-    shards = []
-    for part in (grad_qkv, grad_out):
-        group = lax.axis_size("dp") * seq_count
-        blocks = part.reshape(group, part.shape[0] // group, part.shape[1])
-        shard = lax.psum_scatter(blocks, ("dp", "seq"), scatter_dimension=0, tiled=False)
-        shards.append(shard.astype(jnp.float32))
-    return (
-        outputs.reshape((1,) + out_cotangent.shape),
-        shards[0][None],
-        shards[1][None],
-    )
+    return (outputs.reshape((1,) + out_cotangent.shape), grad_qkv[None], grad_out[None])
 
 
 def solution(mesh):

time: 420 us -> 174 us (0.41)
  waiting for transfers between devices: 277 us -> 0 us
  Pallas kernels: 112 us -> 166 us
  between operations: 14 us -> 0.64 us
  local copies, waits for them, and re-layouts: 14.9 us -> 5.21 us
    unnamed x4 -> x0, waiting for transfers between devices: 277 us -> none
    pallas_call x1, Pallas kernels: 112 us -> 166 us  [relay(): pl.pallas_call(functools.partial(relay_kernel, seq_count, section_count),...]
    reshape x2 -> x0, local copies, waits for them, and re-layouts: 11 us -> none  [local(): blocks = part.reshape(group, part.shape[0] // group, part.shape[1])]
  transfers between devices with their start and end apart: 2 -> 0, of which waited for: 2 -> 0; matrix products, arithmetic and copies ran while one was open for 2% -> 0% of each run, Pallas kernels for 0% -> 0%
where the time goes in v2:
time: 174 us; the launch traced here: 172 us
  Pallas kernels  166 us (95%)
  local copies, waits for them, and re-layouts  5.21 us (3%)
    pallas_call x1, Pallas kernels, relay(): pl.pallas_call(functools.partial(relay_kernel, seq_count, section_count),...  166 us
    unnamed x3, local copies, waits for them, and re-layouts  5.21 us

profile of v2, /device:TPU:2, one launch (start us, length us, event | category | flops | bytes accessed | tf_op | source)
XLA Modules:
  0.0 171.7 jit_solution(15154643487562929504)
XLA Ops:
  0.6 165.9 %relay.1 = (bf16[2,128,1280]{2,1,0:T(8,128)(2,1)}, f32[20,1920]{1,0:T(8,128)}, f32[20,640]{1,0:T(8,128)}) custom-call(bf16[2,128,1280]{2,1,0:T(8,128)(2,1)} %bitcast.12, bf16[1280,1920]{1,0:T(8,128)(2,1)} %bitcast.9, bf16[640,1280]{1,0:T(8,128)(2,1)} %bitcast.10, bf16[2,128,1280]{2,1,0:T(8,128)(2,1)} %bitcast.13), custom_call_target="tpu_custom_call" | custom-call | tf_op jit(solution)/shard_map/relay/pallas_call | solution.py:435
  166.5 1.7 %copy.8 = f32[1,20,1920]{2,0,1:T(1,128)} copy(f32[1,20,1920]{2,1,0:T(8,128)} %bitcast.14) | data formatting | bytes 307200
  168.2 1.5 copy.9
  169.7 2.0 %copy.11 = bf16[1,2,1,128,1280]{4,3,2,1,0:T(8,128)(2,1)} copy(bf16[1,2,1,128,1280]{4,3,2,1,0:T(8,128)(2,1)} %bitcast.11) | data formatting | bytes 1310720

commit v3 on v2

--- a/solution.py
+++ b/solution.py
@@ -63,6 +63,7 @@
     ring_x_recv,
     ring_z_send,
     ring_z_recv,
+    turn,
 ):
     dp_id = lax.axis_index("dp")
     section = lax.axis_index("section")
@@ -166,15 +167,37 @@
     def joined(part):
         return jnp.where(first_head, part[:rows], part[rows:])
 
-    def forward(m, carry):
+    def start_forward(m):
+        for k in range(seq_count):
+            hop(hb, xb, x_send, x_recv, m, k, 1).start()
+
+    def sent_forward(m, first, last):
+        for k in range(first, last):
+            hop(hb, xb, x_send, x_recv, m, k, 1).wait_send()
+
+    def send_in_turns():
+        early = (3 * seq_count) // 4
+        for m in range(micro_count):
+            for c in range(2):
+                turn_id = 2 * m + c
+
+                @pl.when(core == c)
+                def _():
+                    if turn_id > 0:
+                        pl.semaphore_wait(turn.at[turn_id - 1], 1)
+                        start_forward(m)
+                    sent_forward(m, 0, early)
+                    if turn_id < 2 * micro_count - 1:
+                        pl.semaphore_signal(
+                            turn.at[turn_id], inc=1, device_id=other_core, device_id_type=MESH
+                        )
+                    sent_forward(m, early, seq_count)
+
+    def forward(m):
         @pl.when(section > 0)
         def _():
             for k in range(seq_count):
                 arrival(xb, x_recv, m, k).wait()
-
-        @pl.when(is_odd)
-        def _():
-            output_back(m).start()
 
         values = xb[m].astype(jnp.float32)
         centred = values - jnp.mean(values, axis=-1, keepdims=True)
@@ -199,18 +222,23 @@
             )
         hb[m] = (xb[m].astype(jnp.float32) + dot(mx[m], wo[...], 1, 0)).astype(jnp.bfloat16)
 
-        @pl.when(section < section_count - 1)
-        def _():
-            for k in range(seq_count):
-                hop(hb, xb, x_send, x_recv, m, k, 1).start()
+        @pl.when(jnp.logical_and(section > 0, section < section_count - 1))
+        def _():
+            start_forward(m)
+
+        @pl.when(jnp.logical_and(is_first, core + m == 0))
+        def _():
+            start_forward(0)
+
+        @pl.when(jnp.logical_and(is_first, m == micro_count - 1))
+        def _():
+            send_in_turns()
 
         @pl.when(is_odd)
         def _():
             output_own(m).start()
 
-        return carry
-
-    def backward(m, carry):
+    def backward(m):
         @pl.when(section < section_count - 1)
         def _():
             for k in range(seq_count):
@@ -246,21 +274,37 @@
             for k in range(seq_count):
                 hop(bb, gb, g_send, g_recv, m, k, -1).start()
 
-        return carry
-
     @pl.when(is_first)
     def _():
         load_x.wait()
 
     load_wq.wait()
     load_wo.wait()
-    lax.fori_loop(0, micro_count, forward, 0)
 
     @pl.when(is_last)
     def _():
         load_g.wait()
 
-    lax.fori_loop(0, micro_count, backward, 0)
+    def step(t, carry):
+        m = jnp.where(is_last, t // 2, lax.rem(t, micro_count))
+        back = jnp.where(is_last, lax.rem(t, 2), t // micro_count)
+
+        @pl.when(back == 0)
+        def _():
+            forward(m)
+
+        @pl.when(back == 1)
+        def _():
+            backward(m)
+
+        return carry
+
+    lax.fori_loop(0, 2 * micro_count, step, 0)
+
+    @pl.when(is_odd)
+    def _():
+        for m in range(micro_count):
+            output_back(m).start()
 
     tile = 256 if width % 256 == 0 else 128
     tokens = micro_count * rows
@@ -297,15 +341,21 @@
             device_id_type=MESH,
         )
 
-    def reach(count, c, way):
-        return count // 2 if (c + way) % 2 == 0 else count // 2 - 1
-
-    def ring_copy(own, landing, send, recv, c, way, distance, count, me, at):
+    def reach(count, c, way, halved):
+        return count // 2 if halved or (c + way) % 2 == 0 else count // 2 - 1
+
+    def extent(count, way, distance, halved, size):
+        if halved and distance == count // 2:
+            return pl.ds(way * (size // 2), size // 2)
+        return pl.ds(0, size)
+
+    def ring_copy(own, landing, send, recv, c, way, distance, count, me, at, halved):
         step = 1 if way == 0 else -1
         target = lax.rem(me + step * distance + count, count)
+        part = extent(count, way, distance, halved, own.shape[2])
         return pltpu.make_async_remote_copy(
-            src_ref=own.at[c, target],
-            dst_ref=landing.at[c, way, distance - 1],
+            src_ref=own.at[c, target, part, :],
+            dst_ref=landing.at[c, way, distance - 1, part, :],
             send_sem=send.at[c, way, distance - 1],
             recv_sem=recv.at[c, way, distance - 1],
             device_id=at(step),
@@ -314,33 +364,34 @@
 
     def x_copy(c, way, distance):
         return ring_copy(
-            xs, x_in, ring_x_send, ring_x_recv, c, way, distance, x_count, x_id, at_x
+            xs, x_in, ring_x_send, ring_x_recv, c, way, distance, x_count, x_id, at_x, True
         )
 
     def z_copy(c, way, distance):
         return ring_copy(
-            zs, z_in, ring_z_send, ring_z_recv, c, way, distance, seq_count, seq_id, at_z
-        )
-
-    def ring_step(copy, own, landing, count, me, c, distance):
+            zs, z_in, ring_z_send, ring_z_recv, c, way, distance, seq_count, seq_id, at_z, False
+        )
+
+    def ring_step(copy, own, landing, count, me, c, distance, halved):
         for way in range(2):
-            limit = reach(count, c, way)
+            limit = reach(count, c, way, halved)
             if distance > limit:
                 continue
             if distance < limit:
                 copy(c, way, distance + 1).wait_recv()
                 step = 1 if way == 0 else -1
                 target = lax.rem(me + step * distance + count, count)
-                own[c, target] = (
-                    own[c, target].astype(jnp.float32)
-                    + landing[c, way, distance].astype(jnp.float32)
+                part = extent(count, way, distance + 1, halved, own.shape[2])
+                own[c, target, part, :] = (
+                    own[c, target, part, :].astype(jnp.float32)
+                    + landing[c, way, distance, part, :].astype(jnp.float32)
                 ).astype(jnp.bfloat16)
             copy(c, way, distance).start()
 
-    def ring_total(copy, own, landing, count, me, c):
+    def ring_total(copy, own, landing, count, me, c, halved):
         total = own[c, me].astype(jnp.float32)
         for way in range(2):
-            if reach(count, c, way) > 0:
+            if reach(count, c, way, halved) > 0:
                 copy(c, way, 1).wait_recv()
                 total = total + landing[c, way, 0].astype(jnp.float32)
         return total
@@ -357,22 +408,22 @@
                 cw[c, block_rows(x, core), :].astype(jnp.float32)
                 + core_in[c, x].astype(jnp.float32)
             ).astype(jnp.bfloat16)
-        ring_step(x_copy, xs, x_in, x_count, x_id, c, x_count // 2)
+        ring_step(x_copy, xs, x_in, x_count, x_id, c, x_count // 2, True)
 
     def next_x(c, distance):
-        ring_step(x_copy, xs, x_in, x_count, x_id, c, distance)
+        ring_step(x_copy, xs, x_in, x_count, x_id, c, distance, True)
 
     def start_z(c):
-        block_sum[...] = ring_total(x_copy, xs, x_in, x_count, x_id, c)
+        block_sum[...] = ring_total(x_copy, xs, x_in, x_count, x_id, c, True)
         for k in range(seq_count):
             zs[c, k] = block_sum[k * own_rows : (k + 1) * own_rows, :].astype(jnp.bfloat16)
-        ring_step(z_copy, zs, z_in, seq_count, seq_id, c, seq_count // 2)
+        ring_step(z_copy, zs, z_in, seq_count, seq_id, c, seq_count // 2, False)
 
     def next_z(c, distance):
-        ring_step(z_copy, zs, z_in, seq_count, seq_id, c, distance)
+        ring_step(z_copy, zs, z_in, seq_count, seq_id, c, distance, False)
 
     def finish(c):
-        total = ring_total(z_copy, zs, z_in, seq_count, seq_id, c)
+        total = ring_total(z_copy, zs, z_in, seq_count, seq_id, c, False)
         if c < 3:
             grad_qkv_ref[:, c * inner : (c + 1) * inner] = total
         else:
@@ -392,17 +443,16 @@
         for x in range(x_count):
             core_copy(c, x).wait_send()
         for way in range(2):
-            for d in range(1, reach(x_count, c, way) + 1):
+            for d in range(1, reach(x_count, c, way, True) + 1):
                 x_copy(c, way, d).wait_send()
-            for d in range(1, reach(seq_count, c, way) + 1):
+            for d in range(1, reach(seq_count, c, way, False) + 1):
                 z_copy(c, way, d).wait_send()
 
     for m in range(micro_count):
 
-        @pl.when(section < section_count - 1)
-        def _():
-            for k in range(seq_count):
-                hop(hb, xb, x_send, x_recv, m, k, 1).wait_send()
+        @pl.when(jnp.logical_and(section > 0, section < section_count - 1))
+        def _():
+            sent_forward(m, 0, seq_count)
 
         @pl.when(section > 0)
         def _():
@@ -475,6 +525,7 @@
             dma((4, 2, x_count // 2)),
             dma((4, 2, seq_count // 2)),
             dma((4, 2, seq_count // 2)),
+            pltpu.SemaphoreType.REGULAR((2 * micro_count,)),
         ],
         compiler_params=pltpu.CompilerParams(
             collective_id=0, has_side_effects=True, vmem_limit_bytes=60 * 1024 * 1024

time: 174 us -> 160 us (0.920); the launches traced: 172 us -> 160 us
  Pallas kernels: 166 us -> 154 us
    pallas_call x1, Pallas kernels: 166 us -> 154 us  [relay(): pl.pallas_call(functools.partial(relay_kernel, seq_count, section_count),...]
where the time goes in v3:
time: 160 us
  Pallas kernels  154 us (96%)
  local copies, waits for them, and re-layouts  5.21 us (3%)
    pallas_call x1, Pallas kernels, relay(): pl.pallas_call(functools.partial(relay_kernel, seq_count, section_count),...  154 us
    unnamed x3, local copies, waits for them, and re-layouts  5.21 us

profile of v3, /device:TPU:2, one launch (start us, length us, event | category | flops | bytes accessed | tf_op | source)
XLA Modules:
  0.0 159.7 jit_solution(14433072170604168619)
XLA Ops:
  0.6 153.8 %relay.1 = (bf16[2,128,1280]{2,1,0:T(8,128)(2,1)}, f32[20,1920]{1,0:T(8,128)}, f32[20,640]{1,0:T(8,128)}) custom-call(bf16[2,128,1280]{2,1,0:T(8,128)(2,1)} %bitcast.12, bf16[1280,1920]{1,0:T(8,128)(2,1)} %bitcast.9, bf16[640,1280]{1,0:T(8,128)(2,1)} %bitcast.10, bf16[2,128,1280]{2,1,0:T(8,128)(2,1)} %bitcast.13), custom_call_target="tpu_custom_call" | custom-call | tf_op jit(solution)/shard_map/relay/pallas_call | solution.py:485
  154.5 1.7 %copy.8 = f32[1,20,1920]{2,0,1:T(1,128)} copy(f32[1,20,1920]{2,1,0:T(8,128)} %bitcast.14) | data formatting | bytes 307200
  156.2 1.5 copy.9
  157.7 2.0 %copy.11 = bf16[1,2,1,128,1280]{4,3,2,1,0:T(8,128)(2,1)} copy(bf16[1,2,1,128,1280]{4,3,2,1,0:T(8,128)(2,1)} %bitcast.11) | data formatting | bytes 1310720

commit v4 on v3

--- a/solution.py
+++ b/solution.py
@@ -61,9 +61,11 @@
     core_recv,
     ring_x_send,
     ring_x_recv,
-    ring_z_send,
-    ring_z_recv,
+    z_send,
+    z_recv,
     turn,
+    wqt,
+    wot,
 ):
     dp_id = lax.axis_index("dp")
     section = lax.axis_index("section")
@@ -120,10 +122,15 @@
         return (dp_id, section, lax.rem(seq_id + step + seq_count, seq_count))
 
     other_core = (2 * x_id + 1 - core, section, seq_id)
-    for peer in (other_core, at_x(1), at_x(-1), at_z(1), at_z(-1)):
+    peers = [other_core, at_x(1), at_x(-1)] + [at_z(step) for step in range(1, seq_count)]
+    for peer in peers:
         pl.semaphore_signal(barrier, inc=1, device_id=peer, device_id_type=MESH)
-    inner_section = jnp.logical_and(section > 0, section < section_count - 1)
-    pl.semaphore_wait(barrier, jnp.where(inner_section, 2 * seq_count + 5, seq_count + 5))
+
+    def wait_for_peers():
+        inner_section = jnp.logical_and(section > 0, section < section_count - 1)
+        hops = jnp.where(inner_section, 2 * seq_count, seq_count)
+        pl.semaphore_wait(barrier, hops + len(peers))
+
 
     def hop(src, dst, send, recv, m, k, step):
         return pltpu.make_async_remote_copy(
@@ -166,6 +173,46 @@
 
     def joined(part):
         return jnp.where(first_head, part[:rows], part[rows:])
+
+    tile = 256 if width % 256 == 0 else 128
+    tokens = micro_count * rows
+    dp_rows = width // dp_count
+    own_rows = dp_rows // seq_count
+    chunks = 4
+
+    def partial_grads(c):
+        if c < 3:
+            right = dpk[:, :, c * inner : (c + 1) * inner].reshape(tokens, inner)
+            left_ref = nb
+        else:
+            right = mx[...].reshape(tokens, inner)
+            left_ref = gb
+
+        def rows_of(i, carry):
+            cols = pl.ds(pl.multiple_of(i * tile, tile), tile)
+            left = left_ref[:, :, cols].reshape(tokens, tile)
+            cw[c, cols, :] = dot(left, right, 0, 0).astype(jnp.bfloat16)
+            return carry
+
+        lax.fori_loop(0, width // tile, rows_of, 0)
+
+    def block_rows(x, of_core):
+        return pl.ds(pl.multiple_of((2 * x + of_core) * dp_rows, dp_rows), dp_rows)
+
+    def core_copy(c, x):
+        return pltpu.make_async_remote_copy(
+            src_ref=cw.at[c, block_rows(x, 1 - core), :],
+            dst_ref=core_in.at[c, x],
+            send_sem=core_send.at[c, x],
+            recv_sem=core_recv.at[c, x],
+            device_id=other_core,
+            device_id_type=MESH,
+        )
+
+    def start_core(c):
+        partial_grads(c)
+        for x in range(x_count):
+            core_copy(c, x).start()
 
     def start_forward(m):
         for k in range(seq_count):
@@ -222,6 +269,10 @@
             )
         hb[m] = (xb[m].astype(jnp.float32) + dot(mx[m], wo[...], 1, 0)).astype(jnp.bfloat16)
 
+        @pl.when(m == 0)
+        def _():
+            wait_for_peers()
+
         @pl.when(jnp.logical_and(section > 0, section < section_count - 1))
         def _():
             start_forward(m)
@@ -244,7 +295,11 @@
             for k in range(seq_count):
                 arrival(gb, g_recv, m, k).wait()
 
-        d_mixed = dot(gb[m], wo[...], 1, 1).astype(jnp.bfloat16)
+        @pl.when(jnp.logical_and(is_first, m == micro_count - 1))
+        def _():
+            start_core(3)
+
+        d_mixed = dot(gb[m], wot[...], 1, 0).astype(jnp.bfloat16)
         for p in range(pairs):
             query = stacked(pk[m, :, pl.ds(p * 128, 128)])
             key = pk[m, :, pl.ds(inner + p * 128, 128)]
@@ -263,7 +318,7 @@
 
         @pl.when(section > 0)
         def _():
-            d_normed = dot(dpk[m], wq[...], 1, 1)
+            d_normed = dot(dpk[m], wqt[...], 1, 0)
             unit = ub[m]
             d_inside = rb[m, :, 0:1] * (
                 d_normed
@@ -285,7 +340,28 @@
     def _():
         load_g.wait()
 
+    def transpose_weights():
+        def part(i, carry):
+            cols = pl.ds(pl.multiple_of(i * 128, 128), 128)
+            wqt[cols, :] = wq[:, cols].T
+            return carry
+
+        @pl.when(section > 0)
+        def _():
+            lax.fori_loop(0, 3 * inner // 128, part, 0)
+
+        def out_part(i, carry):
+            cols = pl.ds(pl.multiple_of(i * 128, 128), 128)
+            wot[cols, :] = wo[:, cols].T
+            return carry
+
+        lax.fori_loop(0, width // 128, out_part, 0)
+
     def step(t, carry):
+        @pl.when(t == jnp.where(is_last, 0, micro_count))
+        def _():
+            transpose_weights()
+
         m = jnp.where(is_last, t // 2, lax.rem(t, micro_count))
         back = jnp.where(is_last, lax.rem(t, 2), t // micro_count)
 
@@ -306,100 +382,31 @@
         for m in range(micro_count):
             output_back(m).start()
 
-    tile = 256 if width % 256 == 0 else 128
-    tokens = micro_count * rows
-    dp_rows = width // dp_count
-    own_rows = dp_rows // seq_count
-    chunks = 4
-
-    def partial_grads(c):
-        if c < 3:
-            right = dpk[:, :, c * inner : (c + 1) * inner].reshape(tokens, inner)
-            left_ref = nb
-        else:
-            right = mx[...].reshape(tokens, inner)
-            left_ref = gb
-
-        def rows_of(i, carry):
-            cols = pl.ds(pl.multiple_of(i * tile, tile), tile)
-            left = left_ref[:, :, cols].reshape(tokens, tile)
-            cw[c, cols, :] = dot(left, right, 0, 0).astype(jnp.bfloat16)
-            return carry
-
-        lax.fori_loop(0, width // tile, rows_of, 0)
-
-    def block_rows(x, of_core):
-        return pl.ds(pl.multiple_of((2 * x + of_core) * dp_rows, dp_rows), dp_rows)
-
-    def core_copy(c, x):
+    @pl.when(section > 0)
+    def _():
+        start_core(3)
+
+    farthest = x_count // 2
+
+    def x_part(way, distance):
+        if distance == farthest:
+            return pl.ds(way * (dp_rows // 2), dp_rows // 2)
+        return pl.ds(0, dp_rows)
+
+    def x_target(way, distance):
+        step = distance if way == 0 else -distance
+        return lax.rem(x_id + step + x_count, x_count)
+
+    def x_copy(c, way, distance):
+        part = x_part(way, distance)
         return pltpu.make_async_remote_copy(
-            src_ref=cw.at[c, block_rows(x, 1 - core), :],
-            dst_ref=core_in.at[c, x],
-            send_sem=core_send.at[c, x],
-            recv_sem=core_recv.at[c, x],
-            device_id=other_core,
+            src_ref=xs.at[c, x_target(way, distance), part, :],
+            dst_ref=x_in.at[c, way, distance - 1, part, :],
+            send_sem=ring_x_send.at[c, way, distance - 1],
+            recv_sem=ring_x_recv.at[c, way, distance - 1],
+            device_id=at_x(1 if way == 0 else -1),
             device_id_type=MESH,
         )
-
-    def reach(count, c, way, halved):
-        return count // 2 if halved or (c + way) % 2 == 0 else count // 2 - 1
-
-    def extent(count, way, distance, halved, size):
-        if halved and distance == count // 2:
-            return pl.ds(way * (size // 2), size // 2)
-        return pl.ds(0, size)
-
-    def ring_copy(own, landing, send, recv, c, way, distance, count, me, at, halved):
-        step = 1 if way == 0 else -1
-        target = lax.rem(me + step * distance + count, count)
-        part = extent(count, way, distance, halved, own.shape[2])
-        return pltpu.make_async_remote_copy(
-            src_ref=own.at[c, target, part, :],
-            dst_ref=landing.at[c, way, distance - 1, part, :],
-            send_sem=send.at[c, way, distance - 1],
-            recv_sem=recv.at[c, way, distance - 1],
-            device_id=at(step),
-            device_id_type=MESH,
-        )
-
-    def x_copy(c, way, distance):
-        return ring_copy(
-            xs, x_in, ring_x_send, ring_x_recv, c, way, distance, x_count, x_id, at_x, True
-        )
-
-    def z_copy(c, way, distance):
-        return ring_copy(
-            zs, z_in, ring_z_send, ring_z_recv, c, way, distance, seq_count, seq_id, at_z, False
-        )
-
-    def ring_step(copy, own, landing, count, me, c, distance, halved):
-        for way in range(2):
-            limit = reach(count, c, way, halved)
-            if distance > limit:
-                continue
-            if distance < limit:
-                copy(c, way, distance + 1).wait_recv()
-                step = 1 if way == 0 else -1
-                target = lax.rem(me + step * distance + count, count)
-                part = extent(count, way, distance + 1, halved, own.shape[2])
-                own[c, target, part, :] = (
-                    own[c, target, part, :].astype(jnp.float32)
-                    + landing[c, way, distance, part, :].astype(jnp.float32)
-                ).astype(jnp.bfloat16)
-            copy(c, way, distance).start()
-
-    def ring_total(copy, own, landing, count, me, c, halved):
-        total = own[c, me].astype(jnp.float32)
-        for way in range(2):
-            if reach(count, c, way, halved) > 0:
-                copy(c, way, 1).wait_recv()
-                total = total + landing[c, way, 0].astype(jnp.float32)
-        return total
-
-    def start_core(c):
-        partial_grads(c)
-        for x in range(x_count):
-            core_copy(c, x).start()
 
     def start_x(c):
         for x in range(x_count):
@@ -408,45 +415,79 @@
                 cw[c, block_rows(x, core), :].astype(jnp.float32)
                 + core_in[c, x].astype(jnp.float32)
             ).astype(jnp.bfloat16)
-        ring_step(x_copy, xs, x_in, x_count, x_id, c, x_count // 2, True)
+        for way in range(2):
+            x_copy(c, way, farthest).start()
 
     def next_x(c, distance):
-        ring_step(x_copy, xs, x_in, x_count, x_id, c, distance, True)
+        for way in range(2):
+            x_copy(c, way, distance + 1).wait_recv()
+            target = x_target(way, distance)
+            part = x_part(way, distance + 1)
+            xs[c, target, part, :] = (
+                xs[c, target, part, :].astype(jnp.float32)
+                + x_in[c, way, distance, part, :].astype(jnp.float32)
+            ).astype(jnp.bfloat16)
+            x_copy(c, way, distance).start()
+
+    def z_copy(c, step):
+        target = lax.rem(seq_id + step, seq_count)
+        return pltpu.make_async_remote_copy(
+            src_ref=zs.at[c, target],
+            dst_ref=z_in.at[c, seq_id],
+            send_sem=z_send.at[c, step],
+            recv_sem=z_recv.at[c, seq_id],
+            device_id=at_z(step),
+            device_id_type=MESH,
+        )
 
     def start_z(c):
-        block_sum[...] = ring_total(x_copy, xs, x_in, x_count, x_id, c, True)
+        total = xs[c, x_id].astype(jnp.float32)
+        for way in range(2):
+            x_copy(c, way, 1).wait_recv()
+            total = total + x_in[c, way, 0].astype(jnp.float32)
+        block_sum[...] = total
         for k in range(seq_count):
             zs[c, k] = block_sum[k * own_rows : (k + 1) * own_rows, :].astype(jnp.bfloat16)
-        ring_step(z_copy, zs, z_in, seq_count, seq_id, c, seq_count // 2, False)
-
-    def next_z(c, distance):
-        ring_step(z_copy, zs, z_in, seq_count, seq_id, c, distance, False)
+        for step in range(1, seq_count):
+            z_copy(c, step).start()
 
     def finish(c):
-        total = ring_total(z_copy, zs, z_in, seq_count, seq_id, c, False)
+        total = zs[c, seq_id].astype(jnp.float32)
+        for step in range(1, seq_count):
+            source = lax.rem(seq_id + step, seq_count)
+            landed = z_in.at[c, source]
+            pltpu.make_async_copy(landed, landed, z_recv.at[c, source]).wait()
+            total = total + z_in[c, source].astype(jnp.float32)
         if c < 3:
-            grad_qkv_ref[:, c * inner : (c + 1) * inner] = total
+            grad_qkv_ref[:, 0, c * inner : (c + 1) * inner] = total
         else:
-            grad_out_ref[...] = total
-
-    stages = [start_core, start_x]
-    stages += [functools.partial(next_x, distance=d) for d in range(x_count // 2 - 1, 0, -1)]
-    stages += [start_z]
-    stages += [functools.partial(next_z, distance=d) for d in range(seq_count // 2 - 1, 0, -1)]
-    stages += [finish]
-    for tick in range(chunks + len(stages) - 1):
-        for c in range(chunks):
-            if 0 <= tick - c < len(stages):
-                stages[tick - c](c)
+            grad_out_ref[:, 0, :] = total
+
+    start_x(3)
+    start_core(0)
+    start_core(1)
+    start_x(0)
+    start_core(2)
+    start_x(1)
+    order = (3, 0, 1, 2)
+    for distance in range(farthest - 1, 0, -1):
+        for c in order:
+            if c == 0 and distance == farthest - 1:
+                start_x(2)
+            next_x(c, distance)
+    for c in order:
+        start_z(c)
+    for c in order:
+        finish(c)
 
     for c in range(chunks):
         for x in range(x_count):
             core_copy(c, x).wait_send()
         for way in range(2):
-            for d in range(1, reach(x_count, c, way, True) + 1):
+            for d in range(1, farthest + 1):
                 x_copy(c, way, d).wait_send()
-            for d in range(1, reach(seq_count, c, way, False) + 1):
-                z_copy(c, way, d).wait_send()
+        for step in range(1, seq_count):
+            z_copy(c, step).wait_send()
 
     for m in range(micro_count):
 
@@ -486,8 +527,8 @@
         functools.partial(relay_kernel, seq_count, section_count),
         out_shape=(
             jax.ShapeDtypeStruct(tokens, bf16),
-            jax.ShapeDtypeStruct((own_rows, 3 * inner), f32),
-            jax.ShapeDtypeStruct((own_rows, inner), f32),
+            jax.ShapeDtypeStruct((own_rows, 1, 3 * inner), f32),
+            jax.ShapeDtypeStruct((own_rows, 1, inner), f32),
         ),
         in_specs=[any_spec] * 4,
         out_specs=(any_spec, vmem_spec, vmem_spec),
@@ -518,14 +559,16 @@
             pltpu.VMEM((4, 2, x_count // 2, dp_rows, inner), bf16),
             pltpu.VMEM((dp_rows, inner), f32),
             pltpu.VMEM((4, seq_count, own_rows, inner), bf16),
-            pltpu.VMEM((4, 2, seq_count // 2, own_rows, inner), bf16),
+            pltpu.VMEM((4, seq_count, own_rows, inner), bf16),
             dma((4, x_count)),
             dma((4, x_count)),
             dma((4, 2, x_count // 2)),
             dma((4, 2, x_count // 2)),
-            dma((4, 2, seq_count // 2)),
-            dma((4, 2, seq_count // 2)),
+            dma((4, seq_count)),
+            dma((4, seq_count)),
             pltpu.SemaphoreType.REGULAR((2 * micro_count,)),
+            pltpu.VMEM((3 * inner, width), bf16),
+            pltpu.VMEM((width, inner), bf16),
         ],
         compiler_params=pltpu.CompilerParams(
             collective_id=0, has_side_effects=True, vmem_limit_bytes=60 * 1024 * 1024
@@ -541,7 +584,7 @@
     x = clips_in.reshape(micro_count, frames * patches_dev, width)
     g = out_cotangent.reshape(micro_count, -1, width)
     outputs, grad_qkv, grad_out = relay(seq_count, section_count, x, w_qkv[0], w_out[0], g)
-    return (outputs.reshape((1,) + out_cotangent.shape), grad_qkv[None], grad_out[None])
+    return (outputs.reshape((1,) + out_cotangent.shape), grad_qkv.transpose(1, 0, 2), grad_out.transpose(1, 0, 2))
 
 
 def solution(mesh):

time: 160 us -> 148 us (0.925)
  Pallas kernels: 154 us -> 142 us
    pallas_call x1, Pallas kernels: 154 us -> 142 us  [relay(): pl.pallas_call(functools.partial(relay_kernel, seq_count, section_count),...]
where the time goes in v4:
time: 148 us; the launch traced here: 147 us
  Pallas kernels  142 us (96%)
  local copies, waits for them, and re-layouts  5 us (3%)
    pallas_call x1, Pallas kernels, relay(): pl.pallas_call(functools.partial(relay_kernel, seq_count, section_count),...  142 us
    unnamed x3, local copies, waits for them, and re-layouts  5 us

profile of v4, /device:TPU:2, one launch (start us, length us, event | category | flops | bytes accessed | tf_op | source)
XLA Modules:
  0.0 147.4 jit_solution(12629053294452459879)
XLA Ops:
  0.6 141.8 %relay.1 = (bf16[2,128,1280]{2,1,0:T(8,128)(2,1)}, f32[20,1,1920]{2,1,0:T(1,128)}, f32[20,1,640]{2,1,0:T(1,128)}) custom-call(bf16[2,128,1280]{2,1,0:T(8,128)(2,1)} %bitcast.12, bf16[1280,1920]{1,0:T(8,128)(2,1)} %bitcast.9, bf16[640,1280]{1,0:T(8,128)(2,1)} %bitcast.10, bf16[2,128,1280]{2,1,0:T(8,128)(2,1)} %bitcast.13), custom_call_target="tpu_custom_call" | custom-call | tf_op jit(solution)/shard_map/relay/pallas_call | solution.py:526
  142.4 2.0 %copy.11 = bf16[1,2,1,128,1280]{4,3,2,1,0:T(8,128)(2,1)} copy(bf16[1,2,1,128,1280]{4,3,2,1,0:T(8,128)(2,1)} %bitcast.11) | data formatting | bytes 1310720
  144.4 1.6 %copy.12 = f32[1,20,1920]{2,0,1:T(1,128)} copy(f32[1,20,1920]{2,0,1:T(1,128)} %bitcast.14) | data formatting | bytes 307200
  146.0 1.4 copy.13

commit v5 on v4

--- a/solution.py
+++ b/solution.py
@@ -262,7 +262,7 @@
             scores = dot(stacked(query), key, 1, 1) * scale
             scores = jnp.where(same_group, scores, MASKED)
             exps = jnp.exp(scores - jnp.max(scores, axis=-1, keepdims=True))
-            probs = exps / jnp.sum(exps, axis=-1, keepdims=True)
+            probs = exps * (1.0 / jnp.sum(exps, axis=-1, keepdims=True))
             pr[m, p] = probs
             mx[m, :, cols] = joined(dot(probs.astype(jnp.bfloat16), value, 1, 0)).astype(
                 jnp.bfloat16
@@ -577,13 +577,44 @@
     )(x, w_qkv, w_out, g)
 
 
+def hand_over_kernel(*refs):
+    count = (len(refs) - 2) // 3
+    sources, results, buffers = refs[:count], refs[count : 2 * count], refs[2 * count : 3 * count]
+    in_sem, out_sem = refs[3 * count :]
+    loads = [pltpu.make_async_copy(sources[i], buffers[i], in_sem.at[i]) for i in range(count)]
+    stores = [pltpu.make_async_copy(buffers[i], results[i], out_sem.at[i]) for i in range(count)]
+    for load in loads:
+        load.start()
+    for load, store in zip(loads, stores):
+        load.wait()
+        store.start()
+    for store in stores:
+        store.wait()
+
+
+def hand_over(*arrays):
+    count = len(arrays)
+    any_spec = pl.BlockSpec(memory_space=pl.ANY)
+    return pl.pallas_call(
+        hand_over_kernel,
+        out_shape=tuple(jax.ShapeDtypeStruct(a.shape, a.dtype) for a in arrays),
+        in_specs=[any_spec] * count,
+        out_specs=(any_spec,) * count,
+        scratch_shapes=[pltpu.VMEM(a.shape, a.dtype) for a in arrays]
+        + [pltpu.SemaphoreType.DMA((count,)), pltpu.SemaphoreType.DMA((count,))],
+        name="hand_over",
+    )(*arrays)
+
+
 def local(clips_in, w_qkv, w_out, out_cotangent):
     seq_count = lax.axis_size("seq")
     section_count = lax.axis_size("section")
     micro_count, frames, patches_dev, width = clips_in.shape
     x = clips_in.reshape(micro_count, frames * patches_dev, width)
     g = out_cotangent.reshape(micro_count, -1, width)
-    outputs, grad_qkv, grad_out = relay(seq_count, section_count, x, w_qkv[0], w_out[0], g)
+    outputs, grad_qkv, grad_out = hand_over(
+        *relay(seq_count, section_count, x, w_qkv[0], w_out[0], g)
+    )
     return (outputs.reshape((1,) + out_cotangent.shape), grad_qkv.transpose(1, 0, 2), grad_out.transpose(1, 0, 2))
 
 

time: 148 us -> 145 us (0.980)
  local copies, waits for them, and re-layouts: 5 us -> 0 us
  Pallas kernels: 142 us -> 144 us
    unnamed x3 -> x0, local copies, waits for them, and re-layouts: 5 us -> none
    pallas_call x0 -> x1, Pallas kernels: none -> 2.03 us  [hand_over(): pl.pallas_call(hand_over_kernel, out_shape=tuple((jax.ShapeDtypeStruct(a....]
where the time goes in v5:
time: 145 us; the launch traced here: 144 us
  Pallas kernels  144 us (99%)
    pallas_call x1, Pallas kernels, relay(): pl.pallas_call(functools.partial(relay_kernel, seq_count, section_count),...  142 us

profile of v5, /device:TPU:2, one launch (start us, length us, event | category | flops | bytes accessed | tf_op | source)
XLA Modules:
  0.0 144.4 jit_solution(14618613179463234171)
XLA Ops:
  0.6 141.8 %relay.1 = (bf16[2,128,1280]{2,1,0:T(8,128)(2,1)}, f32[20,1,1920]{2,1,0:T(1,128)}, f32[20,1,640]{2,1,0:T(1,128)}) custom-call(bf16[2,128,1280]{2,1,0:T(8,128)(2,1)} %bitcast.11, bf16[1280,1920]{1,0:T(8,128)(2,1)} %bitcast.9, bf16[640,1280]{1,0:T(8,128)(2,1)} %bitcast.10, bf16[2,128,1280]{2,1,0:T(8,128)(2,1)} %bitcast.12), custom_call_target="tpu_custom_call" | custom-call | tf_op jit(solution)/shard_map/relay/pallas_call | solution.py:526
  142.4 2.0 %hand_over.1 = (bf16[2,128,1280]{2,1,0:T(8,128)(2,1)}, f32[20,1,1920]{2,1,0:T(1,128)}, f32[20,1,640]{2,1,0:T(1,128)}) custom-call(bf16[2,128,1280]{2,1,0:T(8,128)(2,1)} %get-tuple-element.9.refs_0_, f32[20,1,1920]{2,1,0:T(1,128)} %get-tuple-element.10.refs_1_, f32[20,1,640]{2,1,0:T(1,128)} %get-tuple-element.11.refs_2_), custom_call_target="tpu_custom_call" | custom-call | tf_op jit(solution)/shard_map/hand_over/pallas_call | solution.py:598
